TPU v7x, 256 devices: a whole 4x4x8 slice. The times are simulated.
256 devices in a mesh: gx: 8 (over z_lo, y), gy: 8 (over z_hi, core), gz: 4 (over x).
Axes of the slice: x: 4, y: 4, z: 8 (z_hi: 4, z_lo: 2; z = z_hi * 2 + z_lo), core: 2. Of those that a mesh axis runs over, the one named last changes fastest.
Arguments:
- e_adjoint: float32 [3, 256, 128, 1024], P(None, 'gx', 'gy', 'gz'), may hold values from -6 to 6
- h_adjoint: float32 [3, 256, 128, 1024], P(None, 'gx', 'gy', 'gz'), may hold values from -6 to 6
- snapshots: bfloat16 [3, 3, 256, 128, 1024], P(None, None, 'gx', 'gy', 'gz'), may hold values from -6 to 6
- material: int32 [256, 128, 1024], P('gx', 'gy', 'gz'), may hold values from 0 to 7
- permittivity: float32 [8], replicated, may hold values from 1 to 12
- design_mask: int32 [256, 128], P('gx', 'gy'), may hold values from 0 to 1
- ports: int32 [3], replicated, may hold values from 0 to 33554431
- amplitudes: float32 [2, 3], replicated, may hold values from -8 to 8
Outputs:
- e_final: float32 [3, 256, 128, 1024], P(None, 'gx', 'gy', 'gz')
- h_final: float32 [3, 256, 128, 1024], P(None, 'gx', 'gy', 'gz')
- gradient: float32 [256, 128], P('gx', ('gy', 'gz'))
All inputs are finite; a program needn't handle non-finite values.
Results may differ from a plain program's by a relative error of at most 0.0003.
Values sent between devices are 32-bit elements; how exact they have to be, the bound alone decides.
A program may use at most 64 MiB of HBM per device.

v0:
```python
import jax
import jax.numpy as jnp
from jax import lax
from jax.sharding import PartitionSpec as P

STEPS = 2


magnetic_step = 0.5
electric_step = 0.5


def from_behind(array, axis, by):
    size = lax.axis_size(axis)
    pairs = [(i, i + by) for i in range(size) if 0 <= i + by < size]
    return lax.ppermute(array, axis, pairs)


def coordinates(anchor, sizes):
    return tuple((anchor[axis] + lax.broadcasted_iota(jnp.int32, sizes, axis) for axis in range(3)))


def port_source(anchor, sizes, port_cells, amp_row):
    cell_x, cell_y, cell_z = coordinates(anchor, sizes)
    source = jnp.zeros(sizes, jnp.float32)
    for port_no in range(port_cells[0].shape[0]):
        struck = (
            (cell_x == port_cells[0][port_no])
            & (cell_y == port_cells[1][port_no])
            & (cell_z == port_cells[2][port_no])
        )
        source = source + jnp.where(struck, amp_row[port_no], 0.0)
    return source


def split_step(electric, magnetic, coef, base, port_cells, amp_row):
    sizes = electric.shape[1:]
    from_x = from_behind(electric[1:3, 0:1], "gx", -1)
    from_y = from_behind(electric[0::2, :, 0:1], "gy", -1)
    from_z = from_behind(electric[0:2, :, :, 0:1], "gz", -1)
    ey_xp = jnp.concatenate([electric[1, 1:], from_x[0]], 0)
    ez_xp = jnp.concatenate([electric[2, 1:], from_x[1]], 0)
    ex_yp = jnp.concatenate([electric[0, :, 1:], from_y[0]], 1)
    ez_yp = jnp.concatenate([electric[2, :, 1:], from_y[1]], 1)
    ex_zp = jnp.concatenate([electric[0, :, :, 1:], from_z[0]], 2)
    ey_zp = jnp.concatenate([electric[1, :, :, 1:], from_z[1]], 2)
    magnetic = jnp.stack(
        [
            magnetic[0] - magnetic_step * (ez_yp - electric[2] - (ey_zp - electric[1])),
            magnetic[1] - magnetic_step * (ex_zp - electric[0] - (ez_xp - electric[2])),
            magnetic[2] - magnetic_step * (ey_xp - electric[1] - (ex_yp - electric[0])),
        ]
    )
    last_x = sizes[0] - 1
    last_y = sizes[1] - 1
    last_z = sizes[2] - 1
    to_x = from_behind(magnetic[1:3, last_x:], "gx", 1)
    to_y = from_behind(magnetic[0::2, :, last_y:], "gy", 1)
    to_z = from_behind(magnetic[0:2, :, :, last_z:], "gz", 1)
    hy_xm = jnp.concatenate([to_x[0], magnetic[1, :last_x]], 0)
    hz_xm = jnp.concatenate([to_x[1], magnetic[2, :last_x]], 0)
    hx_ym = jnp.concatenate([to_y[0], magnetic[0, :, :last_y]], 1)
    hz_ym = jnp.concatenate([to_y[1], magnetic[2, :, :last_y]], 1)
    hx_zm = jnp.concatenate([to_z[0], magnetic[0, :, :, :last_z]], 2)
    hy_zm = jnp.concatenate([to_z[1], magnetic[1, :, :, :last_z]], 2)
    source = port_source(base, sizes, port_cells, amp_row)
    electric = jnp.stack(
        [
            electric[0] + coef * (magnetic[2] - hz_ym - (magnetic[1] - hy_zm)),
            electric[1] + coef * (magnetic[0] - hx_zm - (magnetic[2] - hz_xm)),
            electric[2] + coef * (magnetic[1] - hy_xm - (magnetic[0] - hx_ym)) + source,
        ]
    )
    return (electric, magnetic)


def body(e_adjoint, h_adjoint, snapshots, material, permittivity, design_mask, ports, amplitudes):
    local_x, local_y, local_z = material.shape
    extent = (
        local_x * lax.axis_size("gx"),
        local_y * lax.axis_size("gy"),
        local_z * lax.axis_size("gz"),
    )
    base = (
        lax.axis_index("gx") * local_x,
        lax.axis_index("gy") * local_y,
        lax.axis_index("gz") * local_z,
    )
    plane = extent[1] * extent[2]
    port_cells = (ports // plane, ports // extent[2] % extent[1], ports % extent[2])
    coef = jnp.zeros(material.shape, jnp.float32)
    for material_no in range(permittivity.shape[0]):
        coef = coef + jnp.where(
            material == material_no, electric_step / permittivity[material_no], 0.0
        )
    corr = jnp.zeros(material.shape, jnp.float32)
    electric = e_adjoint
    magnetic = h_adjoint
    for step_no in range(STEPS):
        electric, magnetic = split_step(
            electric, magnetic, coef, base, port_cells, amplitudes[step_no]
        )
        change = snapshots[step_no].astype(jnp.float32) - snapshots[step_no + 1].astype(jnp.float32)
        corr = corr + jnp.sum(electric * change, axis=0)
    column = design_mask.astype(jnp.float32) * jnp.sum(corr, axis=2)
    gradient = lax.psum_scatter(column, "gz", scatter_dimension=1, tiled=True)
    return (electric, magnetic, gradient)


def solution(mesh):
    placed = (
        P(None, "gx", "gy", "gz"),
        P(None, "gx", "gy", "gz"),
        P(None, None, "gx", "gy", "gz"),
        P("gx", "gy", "gz"),
        P(),
        P("gx", "gy"),
        P(),
        P(),
    )
    return jax.shard_map(
        body,
        mesh=mesh,
        in_specs=placed,
        out_specs=(P(None, "gx", "gy", "gz"), P(None, "gx", "gy", "gz"), P("gx", ("gy", "gz"))),
        check_vma=False,
    )
```

profile of v0, /device:TPU:160, one launch (start us, length us, event | category | flops | bytes accessed | tf_op | source)
XLA Modules:
  0.0 138.2 jit_solution(9181375475888648541)
XLA Ops:
  0.6 0.9 slice.323
  1.5 5.4 %collective-permute-start = (f32[2,1,16,256]{3,2,1,0:T(8,128)S(1)}, f32[2,1,16,256]{3,2,1,0:T(8,128)S(1)}, u32[]{:S(2)}, u32[]{:S(2)}) collective-permute-start(f32[2,1,16,256]{3,2,1,0:T(8,128)S(1)} %slice.323), channel_id=1, source_target_pairs={{32,0},{64,32},{96,64},{128,96},{160,128},{192,160},{224,192},{33,... | collective-permute-start | bytes 98312 | tf_op jit(solution)/shard_map/ppermute | solution.py:16
  6.9 1.1 slice.327
  8.0 1.9 %collective-permute-start.1 = (f32[2,32,1,256]{3,1,2,0:T(8,128)S(1)}, f32[2,32,1,256]{3,1,2,0:T(8,128)S(1)}, u32[]{:S(2)}, u32[]{:S(2)}) collective-permute-start(f32[2,32,1,256]{3,1,2,0:T(8,128)S(1)} %copy.478), channel_id=1, source_target_pairs={{4,0},{8,4},{12,8},{16,12},{20,16},{24,20},{28,24},{5,1},{9,5},{13... | collective-permute-start | bytes 196616 | tf_op jit(solution)/shard_map/ppermute | solution.py:16
  9.9 1.1 slice.334
  11.0 1.0 copy.483
  12.0 1.3 collective-permute-start.2
  13.3 0.9 fusion.72
  14.3 1.3 fusion.74
  15.6 0.9 fusion.73
  22.6 2.6 %fusion.70 = (f32[1,32,16,256]{3,2,1,0:T(8,128)}, f32[1,32,16,256]{3,2,1,0:T(8,128)}, f32[1,32,16,256]{3,2,1,0:T(8,128)S(1)}) fusion(f32[3,32,16,256]{3,2,1,0:T(8,128)} %param.9), kind=kLoop, calls=%fused_computation.177 | loop fusion | bytes 3145728 | tf_op jit(solution)/shard_map/slice | solution.py:51
  25.2 1.6 %fusion.69 = (bf16[1,3,32,16,256]{4,3,2,1,0:T(8,128)(2,1)}, bf16[1,3,32,16,256]{4,3,2,1,0:T(8,128)(2,1)}, bf16[1,3,32,16,256]{4,3,2,1,0:T(8,128)(2,1)}) fusion(bf16[3,3,32,16,256]{4,3,2,1,0:T(8,128)(2,1)S(1)} %copy-done.18), kind=kLoop, calls=%fused_computation.176 | loop fusion | bytes 4718592 | tf_op jit(solution)/shard_map/slice | solution.py:103
  27.3 1.3 fusion.56
  29.3 1.1 copy.556
  30.4 1.1 copy.477
  31.5 1.1 copy.555
  32.6 1.1 copy.480
  40.1 1.1 copy.554
  42.6 1.3 slice_bitcast_fusion.38
  44.1 3.6 %fusion.17 = (f32[1,32,16,256]{3,1,2,0:T(8,128)S(1)}, f32[1,32,16,256]{3,1,2,0:T(8,128)S(1)}, f32[1,32,16,256]{3,1,2,0:T(8,128)S(1)}) fusion(f32[1,1,16,256]{3,1,2,0:T(1,128)S(1)} %copy.435, f32[1,31,16,256]{3,1,2,0:T(8,128)S(1)} %copy.552, f32[1,32,1,256]{3,1,2,0:T(8,128)S(1)} %get-tuple-element.74, f32[1,32,15,256]{3,1,2,0:T(8,128)} %copy.477, ...), kind=kLoop, calls=%fused_computation.45 | loop fusion | flops 2752512 | bytes 7864320 | tf_op jit(solution)/shard_map/sub | solution.py:51
  48.3 4.7 %collective-permute-start.4 = (f32[2,32,16,1]{3,1,2,0:T(8,128)S(1)}, f32[2,32,16,1]{3,1,2,0:T(8,128)S(1)}, u32[]{:S(2)}, u32[]{:S(2)}) collective-permute-start(f32[2,32,16,1]{3,1,2,0:T(8,128)S(1)} %pad_maximum_fusion.6), channel_id=1, source_target_pairs={{0,1},{1,2},{2,3},{4,5},{5,6},{6,7},{8,9},{9,10},{10,11},{12,13},{... | collective-permute-start | bytes 12296 | tf_op jit(solution)/shard_map/ppermute | solution.py:16
  53.1 1.9 %collective-permute-start.5 = (f32[2,1,16,256]{3,1,2,0:T(1,128)S(1)}, f32[2,1,16,256]{3,1,2,0:T(1,128)S(1)}, u32[]{:S(2)}, u32[]{:S(2)}) collective-permute-start(f32[2,1,16,256]{3,1,2,0:T(1,128)S(1)} %pad_maximum_fusion.9), channel_id=1, source_target_pairs={{0,32},{32,64},{64,96},{96,128},{128,160},{160,192},{192,224},{1,3... | collective-permute-start | bytes 98312 | tf_op jit(solution)/shard_map/ppermute | solution.py:16
  55.0 2.1 %collective-permute-start.3 = (f32[2,32,1,256]{3,1,2,0:T(8,128)S(1)}, f32[2,32,1,256]{3,1,2,0:T(8,128)S(1)}, u32[]{:S(2)}, u32[]{:S(2)}) collective-permute-start(f32[2,32,1,256]{3,1,2,0:T(8,128)S(1)} %slice.341), channel_id=1, source_target_pairs={{0,4},{4,8},{8,12},{12,16},{16,20},{20,24},{24,28},{1,5},{5,9},{9,... | collective-permute-start | bytes 196616 | tf_op jit(solution)/shard_map/ppermute | solution.py:16
  57.1 7.4 %collective-permute-done.4 = f32[2,32,16,1]{3,1,2,0:T(8,128)S(1)} collective-permute-done((f32[2,32,16,1]{3,1,2,0:T(8,128)S(1)}, f32[2,32,16,1]{3,1,2,0:T(8,128)S(1)}, u32[]{:S(2)}, u32[]{:S(2)}) %collective-permute-start.4) | collective-permute-done | bytes 4128 | tf_op jit(solution)/shard_map/ppermute | solution.py:16
  64.6 2.7 %fusion.29 = (f32[32,16,256]{2,0,1:T(8,128)S(1)}, f32[32,16,256]{2,0,1:T(8,128)S(1)}, f32[32,16,256]{2,0,1:T(8,128)S(1)}) fusion(f32[32,16,255]{2,0,1:T(8,128)S(1)} %get-tuple-element.116, f32[32,16,1]{2,0,1:T(8,128)S(1)} %get-tuple-element.55, f32[31,16,256]{2,0,1:T(8,128)S(1)} %get-tuple-element.115, f32[1,16,256]{2,0,1:T(1,128)S(1)} %get-tuple-element.80, ...), kind=kLoop, calls=%fused_computation.65 | loop fusion | flops 5767168 | bytes 7864352 | tf_op jit(solution)/shard_map/add | solution.py:70
  68.0 1.0 slice_bitcast_fusion.6
  69.0 0.9 slice_bitcast_fusion.8
  70.0 1.8 %fusion.20 = (f32[32,16,256]{2,0,1:T(8,128)S(1)}, f32[32,16,256]{2,0,1:T(8,128)S(1)}) fusion(f32[32,16,256]{2,0,1:T(8,128)S(1)} %get-tuple-element.21, f32[32,15,256]{2,0,1:T(8,128)S(1)} %get-tuple-element.119, f32[32,1,256]{2,0,1:T(8,128)S(1)} %get-tuple-element.70, f32[32,16,255]{2,0,1:T(8,128)S(1)} %get-tuple-element.117, ...), kind=kLoop, calls=%fused_computation.50 | loop fusion | flops 4849664 | bytes 5767200 | tf_op jit(solution)/shard_map/add | solution.py:69
  71.9 3.1 %fusion.33 = f32[32,16,256]{2,0,1:T(8,128)S(1)} fusion(f32[32,16,256]{2,0,1:T(8,128)S(1)} %get-tuple-element.24, f32[31,16,256]{2,0,1:T(8,128)S(1)} %get-tuple-element.114, f32[1,16,256]{2,0,1:T(1,128)S(1)} %get-tuple-element.79, f32[32,16,256]{2,0,1:T(8,128)S(1)} %get-tuple-element.22, f32[32,15,256]{2,0,1:T(8,128)S(1)} %get-tuple-element.118, ...), kind=kLoop, calls=%fused_computation.71 | loop fusion | flops 5505024 | bytes 3670972 | tf_op jit(solution)/shard_map/add | solution.py:71
  75.8 0.9 slice_bitcast_fusion.4
  78.2 1.0 slice_bitcast_fusion.5
  79.4 1.3 collective-permute-start.8
  81.3 2.6 %collective-permute-start.6 = (f32[2,1,16,256]{3,1,2,0:T(1,128)}, f32[2,1,16,256]{3,1,2,0:T(1,128)}, u32[]{:S(2)}, u32[]{:S(2)}) collective-permute-start(f32[2,1,16,256]{3,1,2,0:T(1,128)} %pad_maximum_fusion.8), channel_id=1, source_target_pairs={{32,0},{64,32},{96,64},{128,96},{160,128},{192,160},{224,192},{33,... | collective-permute-start | bytes 98312 | tf_op jit(solution)/shard_map/ppermute | solution.py:16
  84.0 1.9 %collective-permute-start.7 = (f32[2,32,1,256]{3,1,2,0:T(8,128)S(1)}, f32[2,32,1,256]{3,1,2,0:T(8,128)S(1)}, u32[]{:S(2)}, u32[]{:S(2)}) collective-permute-start(f32[2,32,1,256]{3,1,2,0:T(8,128)S(1)} %slice.372), channel_id=1, source_target_pairs={{4,0},{8,4},{12,8},{16,12},{20,16},{24,20},{28,24},{5,1},{9,5},{13... | collective-permute-start | bytes 196616 | tf_op jit(solution)/shard_map/ppermute | solution.py:16
  85.9 9.3 %collective-permute-done.8 = f32[2,32,16,1]{3,2,1,0:T(8,128)S(1)} collective-permute-done((f32[2,32,16,1]{3,2,1,0:T(8,128)S(1)}, f32[2,32,16,1]{3,2,1,0:T(8,128)S(1)}, u32[]{:S(2)}, u32[]{:S(2)}) %collective-permute-start.8) | collective-permute-done | bytes 4128 | tf_op jit(solution)/shard_map/ppermute | solution.py:16
  95.9 1.1 copy.451
  97.4 0.9 copy.452
  99.1 3.1 %fusion.39 = (f32[32,16,256]{2,0,1:T(8,128)S(1)}, f32[32,16,256]{2,0,1:T(8,128)S(1)}, f32[32,16,256]{2,0,1:T(8,128)S(1)}) fusion(f32[32,16,256]{2,0,1:T(8,128)} %copy-done.9, f32[32,16,256]{2,0,1:T(8,128)S(1)} %fusion.33, f32[32,1,256]{2,0,1:T(8,128)S(1)} %get-tuple-element.67, f32[32,15,256]{2,0,1:T(8,128)} %slice_bitcast_fusion.14, ...), kind=kLoop, calls=%fused_computation.81 | loop fusion | flops 2752512 | bytes 7864320 | tf_op jit(solution)/shard_map/sub | solution.py:49
  102.9 3.7 %collective-permute-start.10 = (f32[2,32,16,1]{3,1,2,0:T(8,128)S(1)}, f32[2,32,16,1]{3,1,2,0:T(8,128)S(1)}, u32[]{:S(2)}, u32[]{:S(2)}) collective-permute-start(f32[2,32,16,1]{3,1,2,0:T(8,128)S(1)} %pad_maximum_fusion.4), channel_id=1, source_target_pairs={{0,1},{1,2},{2,3},{4,5},{5,6},{6,7},{8,9},{9,10},{10,11},{12,13},{... | collective-permute-start | bytes 12296 | tf_op jit(solution)/shard_map/ppermute | solution.py:16
  106.6 2.1 %copy.471 = f32[3,32,16,256]{3,2,1,0:T(8,128)} copy(f32[3,32,16,256]{3,1,2,0:T(8,128)S(1)} %pad_maximum_fusion.2) | data formatting | bytes 3145728
  108.7 1.9 %collective-permute-start.11 = (f32[2,1,16,256]{3,1,2,0:T(1,128)S(1)}, f32[2,1,16,256]{3,1,2,0:T(1,128)S(1)}, u32[]{:S(2)}, u32[]{:S(2)}) collective-permute-start(f32[2,1,16,256]{3,1,2,0:T(1,128)S(1)} %pad_maximum_fusion.7), channel_id=1, source_target_pairs={{0,32},{32,64},{64,96},{96,128},{128,160},{160,192},{192,224},{1,3... | collective-permute-start | bytes 98312 | tf_op jit(solution)/shard_map/ppermute | solution.py:16
  110.6 2.1 %collective-permute-start.9 = (f32[2,32,1,256]{3,1,2,0:T(8,128)S(1)}, f32[2,32,1,256]{3,1,2,0:T(8,128)S(1)}, u32[]{:S(2)}, u32[]{:S(2)}) collective-permute-start(f32[2,32,1,256]{3,1,2,0:T(8,128)S(1)} %slice.383), channel_id=1, source_target_pairs={{0,4},{4,8},{8,12},{12,16},{16,20},{20,24},{24,28},{1,5},{5,9},{9,... | collective-permute-start | bytes 196616 | tf_op jit(solution)/shard_map/ppermute | solution.py:16
  112.7 3.6 %collective-permute-done.10 = f32[2,32,16,1]{3,1,2,0:T(8,128)S(1)} collective-permute-done((f32[2,32,16,1]{3,1,2,0:T(8,128)S(1)}, f32[2,32,16,1]{3,1,2,0:T(8,128)S(1)}, u32[]{:S(2)}, u32[]{:S(2)}) %collective-permute-start.10) | collective-permute-done | bytes 4128 | tf_op jit(solution)/shard_map/ppermute | solution.py:16
  117.3 1.0 collective-permute-done.9
  119.2 2.8 %fusion.55 = f32[1,32,16,256]{3,1,2,0:T(8,128)S(1)} fusion(f32[32,16,256]{2,0,1:T(8,128)S(1)} %fusion.33, f32[32,16,256]{2,0,1:T(8,128)S(1)} %get-tuple-element.45, f32[31,16,256]{2,0,1:T(8,128)S(1)} %slice_bitcast_fusion, f32[1,16,256]{2,0,1:T(1,128)S(1)} %get-tuple-element.76, f32[32,16,256]{2,0,1:T(8,128)S(1)} %get-tuple-element.43, ...), kind=kLoop, calls=%fused_computation.105 | loop fusion | flops 5505024 | bytes 3670972 | tf_op jit(solution)/shard_map/stack | solution.py:67
  122.0 2.3 %fusion.5 = (f32[32,16,256]{2,0,1:T(8,128)S(1)}, f32[32,16,256]{2,0,1:T(8,128)S(1)}, f32[3,32,16,256]{3,1,2,0:T(8,128)}) fusion(bf16[1,3,32,16,256]{4,3,2,1,0:T(8,128)(2,1)S(1)} %copy-done.17, bf16[1,3,32,16,256]{4,3,2,1,0:T(8,128)(2,1)S(1)} %copy-done.16, f32[1,32,16,256]{3,1,2,0:T(8,128)S(1)} %fusion.55, f32[1,32,16,256]{3,1,2,0:T(8,128)S(1)} %fusion.50, ...), kind=kLoop, calls=%fused_computation.7 | loop fusion | flops 4849664 | bytes 8126464 | tf_op jit(solution)/shard_map/reduce_sum | solution.py:104
  124.6 9.6 %all-reduce = f32[32,16]{0,1:T(8,128)S(1)} all-reduce(f32[32,16]{0,1:T(8,128)S(1)} %convert_multiply_fusion), channel_id=2, replica_groups=mesh['gx'=8,'gy'=8,'gz'=4] {'gz'}, use_global_device_ids=true, to_apply=%region_3.4.clone | all-reduce | flops 512 | bytes 4096
  134.1 3.5 %copy.470 = f32[3,32,16,256]{3,2,1,0:T(8,128)} copy(f32[3,32,16,256]{3,1,2,0:T(8,128)} %get-tuple-element.28) | data formatting | bytes 3145728
  (169 shorter events, 18.4 us)
Async XLA Ops:
  0.6 12.6 %copy-start.1 = (f32[3,32,16,256]{3,2,1,0:T(8,128)S(1)}, f32[3,32,16,256]{3,2,1,0:T(8,128)}, u32[]{:S(2)}) copy-start(f32[3,32,16,256]{3,2,1,0:T(8,128)} %param.8) | copy-start | bytes 4718596
  1.5 42.3 %collective-permute-start = (f32[2,1,16,256]{3,2,1,0:T(8,128)S(1)}, f32[2,1,16,256]{3,2,1,0:T(8,128)S(1)}, u32[]{:S(2)}, u32[]{:S(2)}) collective-permute-start(f32[2,1,16,256]{3,2,1,0:T(8,128)S(1)} %slice.323), channel_id=1, source_target_pairs={{32,0},{64,32},{96,64},{128,96},{160,128},{192,160},{224,192},{33,... | collective-permute-start | bytes 98312 | tf_op jit(solution)/shard_map/ppermute | solution.py:16
  8.0 36.0 %collective-permute-start.1 = (f32[2,32,1,256]{3,1,2,0:T(8,128)S(1)}, f32[2,32,1,256]{3,1,2,0:T(8,128)S(1)}, u32[]{:S(2)}, u32[]{:S(2)}) collective-permute-start(f32[2,32,1,256]{3,1,2,0:T(8,128)S(1)} %copy.478), channel_id=1, source_target_pairs={{4,0},{8,4},{12,8},{16,12},{20,16},{24,20},{28,24},{5,1},{9,5},{13... | collective-permute-start | bytes 196616 | tf_op jit(solution)/shard_map/ppermute | solution.py:16
  12.0 30.6 %collective-permute-start.2 = (f32[2,32,16,1]{3,1,2,0:T(8,128)}, f32[2,32,16,1]{3,1,2,0:T(8,128)}, u32[]{:S(2)}, u32[]{:S(2)}) collective-permute-start(f32[2,32,16,1]{3,1,2,0:T(8,128)} %copy.483), channel_id=1, source_target_pairs={{1,0},{2,1},{3,2},{5,4},{6,5},{7,6},{9,8},{10,9},{11,10},{13,12},{... | collective-permute-start | bytes 12296 | tf_op jit(solution)/shard_map/ppermute | solution.py:16
  15.6 5.6 %copy-start.25 = (f32[2,3]{1,0:T(2,128)S(1)}, f32[2,3]{1,0:T(2,128)}, u32[]{:S(2)}) copy-start(f32[2,3]{1,0:T(2,128)} %param.15) | copy-start | bytes 76
  15.6 6.3 %copy-start.24 = (f32[8]{0:T(128)S(1)}, f32[8]{0:T(128)}, u32[]{:S(2)}) copy-start(f32[8]{0:T(128)} %param.12) | copy-start | bytes 100
  18.5 53.3 %copy-start.31 = (pred[32]{0:T(512)(128)(4,1)}, pred[32]{0:T(512)(128)(4,1)S(1)}, u32[]{:S(2)}) copy-start(pred[32]{0:T(512)(128)(4,1)S(1)} %fusion.65) | copy-start | bytes 100
  19.2 52.6 %copy-start.33 = (pred[32]{0:T(512)(128)(4,1)}, pred[32]{0:T(512)(128)(4,1)S(1)}, u32[]{:S(2)}) copy-start(pred[32]{0:T(512)(128)(4,1)S(1)} %fusion.63) | copy-start | bytes 100
  19.8 52.0 %copy-start.35 = (pred[32]{0:T(512)(128)(4,1)}, pred[32]{0:T(512)(128)(4,1)S(1)}, u32[]{:S(2)}) copy-start(pred[32]{0:T(512)(128)(4,1)S(1)} %fusion.64) | copy-start | bytes 100
  20.5 51.3 %copy-start.37 = (pred[16]{0:T(512)(128)(4,1)}, pred[16]{0:T(512)(128)(4,1)S(1)}, u32[]{:S(2)}) copy-start(pred[16]{0:T(512)(128)(4,1)S(1)} %fusion.61) | copy-start | bytes 52
  21.2 50.6 %copy-start.39 = (pred[16]{0:T(512)(128)(4,1)}, pred[16]{0:T(512)(128)(4,1)S(1)}, u32[]{:S(2)}) copy-start(pred[16]{0:T(512)(128)(4,1)S(1)} %fusion.60) | copy-start | bytes 52
  22.6 2.6 %copy-start.18 = (bf16[3,3,32,16,256]{4,3,2,1,0:T(8,128)(2,1)S(1)}, bf16[3,3,32,16,256]{4,3,2,1,0:T(8,128)(2,1)}, u32[]{:S(2)}) copy-start(bf16[3,3,32,16,256]{4,3,2,1,0:T(8,128)(2,1)} %param.10) | copy-start | bytes 7077892
  25.2 18.8 %copy-start.7 = (f32[1,32,16,256]{3,2,1,0:T(8,128)}, f32[1,32,16,256]{3,2,1,0:T(8,128)S(1)}, u32[]{:S(2)}) copy-start(f32[1,32,16,256]{3,2,1,0:T(8,128)S(1)} %get-tuple-element.31) | copy-start | bytes 1572868
  27.3 44.5 %copy-start.41 = (pred[256]{0:T(512)(128)(4,1)}, pred[256]{0:T(512)(128)(4,1)S(1)}, u32[]{:S(2)}) copy-start(pred[256]{0:T(512)(128)(4,1)S(1)} %fusion.58) | copy-start | bytes 772
  28.6 43.2 %copy-start.27 = (pred[256]{0:T(512)(128)(4,1)}, pred[256]{0:T(512)(128)(4,1)S(1)}, u32[]{:S(2)}) copy-start(pred[256]{0:T(512)(128)(4,1)S(1)} %get-tuple-element.120) | copy-start | bytes 772
  28.6 43.2 %copy-start.29 = (pred[256]{0:T(512)(128)(4,1)}, pred[256]{0:T(512)(128)(4,1)S(1)}, u32[]{:S(2)}) copy-start(pred[256]{0:T(512)(128)(4,1)S(1)} %get-tuple-element.121) | copy-start | bytes 772
  29.3 42.6 %copy-start.43 = (pred[16]{0:T(512)(128)(4,1)}, pred[16]{0:T(512)(128)(4,1)S(1)}, u32[]{:S(2)}) copy-start(pred[16]{0:T(512)(128)(4,1)S(1)} %fusion.62) | copy-start | bytes 52
  30.4 8.7 %copy-start.21 = (f32[1,31,16,256]{3,2,1,0:T(8,128)S(1)}, f32[1,31,16,256]{3,2,1,0:T(8,128)}, u32[]{:S(2)}) copy-start(f32[1,31,16,256]{3,2,1,0:T(8,128)} %get-tuple-element.34) | copy-start | bytes 1523716
  32.6 7.2 %copy-start.20 = (f32[1,32,16,255]{3,2,1,0:T(8,128)S(1)}, f32[1,32,16,255]{3,2,1,0:T(8,128)}, u32[]{:S(2)}) copy-start(f32[1,32,16,255]{3,2,1,0:T(8,128)} %get-tuple-element.39) | copy-start | bytes 1566724
  34.3 5.8 %copy-start.19 = (f32[1,32,16,255]{3,2,1,0:T(8,128)S(1)}, f32[1,32,16,255]{3,2,1,0:T(8,128)}, u32[]{:S(2)}) copy-start(f32[1,32,16,255]{3,2,1,0:T(8,128)} %get-tuple-element.40) | copy-start | bytes 1566724
  39.4 1.8 %copy-start.46 = (u32[256]{0:T(256)S(1)}, u32[256]{0:T(256)}, u32[]{:S(2)}) copy-start(u32[256]{0:T(256)} %constant.99) | copy-start | bytes 3076
  39.7 4.3 %copy-start.3 = (f32[1,31,16,256]{3,1,2,0:T(8,128)}, f32[1,31,16,256]{3,1,2,0:T(8,128)S(1)}, u32[]{:S(2)}) copy-start(f32[1,31,16,256]{3,1,2,0:T(8,128)S(1)} %copy.551) | copy-start | bytes 1523716
  40.1 7.5 %copy-start.5 = (f32[1,32,16,255]{3,1,2,0:T(8,128)}, f32[1,32,16,255]{3,1,2,0:T(8,128)S(1)}, u32[]{:S(2)}) copy-start(f32[1,32,16,255]{3,1,2,0:T(8,128)S(1)} %copy.553) | copy-start | bytes 1566724
  42.5 1.5 %copy-start.10 = (f32[1,32,16,255]{3,1,2,0:T(8,128)S(1)}, f32[1,32,16,255]{3,1,2,0:T(8,128)}, u32[]{:S(2)}) copy-start(f32[1,32,16,255]{3,1,2,0:T(8,128)} %copy.554) | copy-start | bytes 1566724
  42.6 1.5 %copy-start.12 = (f32[1,32,16,256]{3,2,1,0:T(8,128)S(1)}, f32[1,32,16,256]{3,2,1,0:T(8,128)}, u32[]{:S(2)}) copy-start(f32[1,32,16,256]{3,2,1,0:T(8,128)} %get-tuple-element.29) | copy-start | bytes 1572868
  48.3 16.3 %copy-start = (s32[32,16,256]{2,1,0:T(8,128)S(1)}, s32[32,16,256]{2,1,0:T(8,128)}, u32[]{:S(2)}) copy-start(s32[32,16,256]{2,1,0:T(8,128)} %param.11) | copy-start | bytes 1572868
  48.3 16.3 %copy-start.13 = (f32[1,32,16,256]{3,2,1,0:T(8,128)S(1)}, f32[1,32,16,256]{3,2,1,0:T(8,128)}, u32[]{:S(2)}) copy-start(f32[1,32,16,256]{3,2,1,0:T(8,128)} %get-tuple-element.30) | copy-start | bytes 1572868
  48.3 16.3 %copy-start.22 = (f32[1,32,15,256]{3,1,2,0:T(8,128)S(1)}, f32[1,32,15,256]{3,1,2,0:T(8,128)}, u32[]{:S(2)}) copy-start(f32[1,32,15,256]{3,1,2,0:T(8,128)} %copy.556) | copy-start | bytes 1474564
  48.3 16.3 %copy-start.23 = (f32[1,32,15,256]{3,1,2,0:T(8,128)S(1)}, f32[1,32,15,256]{3,1,2,0:T(8,128)}, u32[]{:S(2)}) copy-start(f32[1,32,15,256]{3,1,2,0:T(8,128)} %copy.555) | copy-start | bytes 1474564
  48.3 16.2 %collective-permute-start.4 = (f32[2,32,16,1]{3,1,2,0:T(8,128)S(1)}, f32[2,32,16,1]{3,1,2,0:T(8,128)S(1)}, u32[]{:S(2)}, u32[]{:S(2)}) collective-permute-start(f32[2,32,16,1]{3,1,2,0:T(8,128)S(1)} %pad_maximum_fusion.6), channel_id=1, source_target_pairs={{0,1},{1,2},{2,3},{4,5},{5,6},{6,7},{8,9},{9,10},{10,11},{12,13},{... | collective-permute-start | bytes 12296 | tf_op jit(solution)/shard_map/ppermute | solution.py:16
  53.1 11.5 %collective-permute-start.5 = (f32[2,1,16,256]{3,1,2,0:T(1,128)S(1)}, f32[2,1,16,256]{3,1,2,0:T(1,128)S(1)}, u32[]{:S(2)}, u32[]{:S(2)}) collective-permute-start(f32[2,1,16,256]{3,1,2,0:T(1,128)S(1)} %pad_maximum_fusion.9), channel_id=1, source_target_pairs={{0,32},{32,64},{64,96},{96,128},{128,160},{160,192},{192,224},{1,3... | collective-permute-start | bytes 98312 | tf_op jit(solution)/shard_map/ppermute | solution.py:16
  55.0 14.9 %collective-permute-start.3 = (f32[2,32,1,256]{3,1,2,0:T(8,128)S(1)}, f32[2,32,1,256]{3,1,2,0:T(8,128)S(1)}, u32[]{:S(2)}, u32[]{:S(2)}) collective-permute-start(f32[2,32,1,256]{3,1,2,0:T(8,128)S(1)} %slice.341), channel_id=1, source_target_pairs={{0,4},{4,8},{8,12},{12,16},{16,20},{20,24},{24,28},{1,5},{5,9},{9,... | collective-permute-start | bytes 196616 | tf_op jit(solution)/shard_map/ppermute | solution.py:16
  67.3 2.6 %copy-start.14 = (f32[32,16,256]{2,0,1:T(8,128)}, f32[32,16,256]{2,0,1:T(8,128)S(1)}, u32[]{:S(2)}) copy-start(f32[32,16,256]{2,0,1:T(8,128)S(1)} %get-tuple-element.21) | copy-start | bytes 1572868
  67.4 4.5 %copy-start.9 = (f32[32,16,256]{2,0,1:T(8,128)}, f32[32,16,256]{2,0,1:T(8,128)S(1)}, u32[]{:S(2)}) copy-start(f32[32,16,256]{2,0,1:T(8,128)S(1)} %get-tuple-element.22) | copy-start | bytes 1572868
  67.7 2.2 %copy-start.4 = (f32[1,31,16,256]{3,1,2,0:T(8,128)S(1)}, f32[1,31,16,256]{3,1,2,0:T(8,128)}, u32[]{:S(2)}) copy-start(f32[1,31,16,256]{3,1,2,0:T(8,128)} %copy-done.3) | copy-start | bytes 1523716
  67.7 2.2 %copy-start.6 = (f32[1,32,16,255]{3,1,2,0:T(8,128)S(1)}, f32[1,32,16,255]{3,1,2,0:T(8,128)}, u32[]{:S(2)}) copy-start(f32[1,32,16,255]{3,1,2,0:T(8,128)} %copy-done.5) | copy-start | bytes 1566724
  67.7 2.2 %copy-start.8 = (f32[1,32,16,256]{3,2,1,0:T(8,128)S(1)}, f32[1,32,16,256]{3,2,1,0:T(8,128)}, u32[]{:S(2)}) copy-start(f32[1,32,16,256]{3,2,1,0:T(8,128)} %copy-done.7) | copy-start | bytes 1572868
  71.8 3.2 %copy-start.2 = (f32[32,16,256]{2,0,1:T(8,128)}, f32[32,16,256]{2,0,1:T(8,128)S(1)}, u32[]{:S(2)}) copy-start(f32[32,16,256]{2,0,1:T(8,128)S(1)} %get-tuple-element.24) | copy-start | bytes 1572868
  79.4 15.8 %collective-permute-start.8 = (f32[2,32,16,1]{3,2,1,0:T(8,128)S(1)}, f32[2,32,16,1]{3,2,1,0:T(8,128)S(1)}, u32[]{:S(2)}, u32[]{:S(2)}) collective-permute-start(f32[2,32,16,1]{3,2,1,0:T(8,128)S(1)} %pad_maximum_fusion.5), channel_id=1, source_target_pairs={{1,0},{2,1},{3,2},{5,4},{6,5},{7,6},{9,8},{10,9},{11,10},{13,12},{... | collective-permute-start | bytes 12296 | tf_op jit(solution)/shard_map/ppermute | solution.py:16
  81.3 17.0 %collective-permute-start.6 = (f32[2,1,16,256]{3,1,2,0:T(1,128)}, f32[2,1,16,256]{3,1,2,0:T(1,128)}, u32[]{:S(2)}, u32[]{:S(2)}) collective-permute-start(f32[2,1,16,256]{3,1,2,0:T(1,128)} %pad_maximum_fusion.8), channel_id=1, source_target_pairs={{32,0},{64,32},{96,64},{128,96},{160,128},{192,160},{224,192},{33,... | collective-permute-start | bytes 98312 | tf_op jit(solution)/shard_map/ppermute | solution.py:16
  84.0 15.1 %collective-permute-start.7 = (f32[2,32,1,256]{3,1,2,0:T(8,128)S(1)}, f32[2,32,1,256]{3,1,2,0:T(8,128)S(1)}, u32[]{:S(2)}, u32[]{:S(2)}) collective-permute-start(f32[2,32,1,256]{3,1,2,0:T(8,128)S(1)} %slice.372), channel_id=1, source_target_pairs={{4,0},{8,4},{12,8},{16,12},{20,16},{24,20},{28,24},{5,1},{9,5},{13... | collective-permute-start | bytes 196616 | tf_op jit(solution)/shard_map/ppermute | solution.py:16
  102.9 13.5 %collective-permute-start.10 = (f32[2,32,16,1]{3,1,2,0:T(8,128)S(1)}, f32[2,32,16,1]{3,1,2,0:T(8,128)S(1)}, u32[]{:S(2)}, u32[]{:S(2)}) collective-permute-start(f32[2,32,16,1]{3,1,2,0:T(8,128)S(1)} %pad_maximum_fusion.4), channel_id=1, source_target_pairs={{0,1},{1,2},{2,3},{4,5},{5,6},{6,7},{8,9},{9,10},{10,11},{12,13},{... | collective-permute-start | bytes 12296 | tf_op jit(solution)/shard_map/ppermute | solution.py:16
  108.7 7.9 %collective-permute-start.11 = (f32[2,1,16,256]{3,1,2,0:T(1,128)S(1)}, f32[2,1,16,256]{3,1,2,0:T(1,128)S(1)}, u32[]{:S(2)}, u32[]{:S(2)}) collective-permute-start(f32[2,1,16,256]{3,1,2,0:T(1,128)S(1)} %pad_maximum_fusion.7), channel_id=1, source_target_pairs={{0,32},{32,64},{64,96},{96,128},{128,160},{160,192},{192,224},{1,3... | collective-permute-start | bytes 98312 | tf_op jit(solution)/shard_map/ppermute | solution.py:16
  110.6 7.7 %collective-permute-start.9 = (f32[2,32,1,256]{3,1,2,0:T(8,128)S(1)}, f32[2,32,1,256]{3,1,2,0:T(8,128)S(1)}, u32[]{:S(2)}, u32[]{:S(2)}) collective-permute-start(f32[2,32,1,256]{3,1,2,0:T(8,128)S(1)} %slice.383), channel_id=1, source_target_pairs={{0,4},{4,8},{8,12},{12,16},{16,20},{20,24},{24,28},{1,5},{5,9},{9,... | collective-permute-start | bytes 196616 | tf_op jit(solution)/shard_map/ppermute | solution.py:16
  119.1 2.9 %copy-start.15 = (bf16[1,3,32,16,256]{4,3,2,1,0:T(8,128)(2,1)S(1)}, bf16[1,3,32,16,256]{4,3,2,1,0:T(8,128)(2,1)}, u32[]{:S(2)}) copy-start(bf16[1,3,32,16,256]{4,3,2,1,0:T(8,128)(2,1)} %get-tuple-element.25) | copy-start | bytes 2359300
  119.1 2.9 %copy-start.16 = (bf16[1,3,32,16,256]{4,3,2,1,0:T(8,128)(2,1)S(1)}, bf16[1,3,32,16,256]{4,3,2,1,0:T(8,128)(2,1)}, u32[]{:S(2)}) copy-start(bf16[1,3,32,16,256]{4,3,2,1,0:T(8,128)(2,1)} %get-tuple-element.26) | copy-start | bytes 2359300
  119.2 2.9 %copy-start.17 = (bf16[1,3,32,16,256]{4,3,2,1,0:T(8,128)(2,1)S(1)}, bf16[1,3,32,16,256]{4,3,2,1,0:T(8,128)(2,1)}, u32[]{:S(2)}) copy-start(bf16[1,3,32,16,256]{4,3,2,1,0:T(8,128)(2,1)} %get-tuple-element.27) | copy-start | bytes 2359300
  122.0 2.5 %copy-start.26 = (s32[32,16]{0,1:T(8,128)S(1)}, s32[32,16]{0,1:T(8,128)}, u32[]{:S(2)}) copy-start(s32[32,16]{0,1:T(8,128)} %param.13) | copy-start | bytes 6148
  (11 other events, 9.4 us)
where the time goes:
time: 140 us; the launch traced here: 138 us
  local copies, waits for them, and re-layouts  39.9 us (28%)
  starting transfers between devices  30.9 us (22%)
  other arithmetic  28.5 us (20%)
  waiting for transfers between devices  21.5 us (15%)
  blocking collectives  9.59 us (7%)
  between operations  7.9 us (6%)
    ppermute x12, starting transfers between devices, from_behind(): return lax.ppermute(array, axis, pairs)  30.9 us
    ppermute x12, waiting for transfers between devices, from_behind(): return lax.ppermute(array, axis, pairs)  21.5 us
    unnamed x104, local copies, waits for them, and re-layouts  12.3 us
    unnamed x1, blocking collectives  9.59 us
    another operation x6, other arithmetic, split_step(): jnp.stack([electric[0] + coef * (magnetic[2] - hz_ym - (magnetic[1] - hy_...  5.04 us
    sub x1, other arithmetic, split_step(): magnetic[2] - magnetic_step * (ey_xp - electric[1] - (ex_yp - electric[0]))  3.55 us
    sub x1, other arithmetic, split_step(): magnetic[0] - magnetic_step * (ez_yp - electric[2] - (ey_zp - electric[1]))  3.14 us
    add x1, other arithmetic, split_step(): electric[2] + coef * (magnetic[1] - hy_xm - (magnetic[0] - hx_ym)) + source  3.1 us
  transfers between devices with their start and end apart: 12, of which 5 were waited for; matrix products, arithmetic and copies ran while one was open for 29% of the time, Pallas kernels for 0%

commit v1 on v0

v1 whole, which is shorter than its diff:
```python
import jax
import jax.numpy as jnp
from jax import lax
from jax.experimental import pallas as pl
from jax.experimental.pallas import tpu as pltpu
from jax.sharding import PartitionSpec as P

STEPS = 2
AXES = ("gx", "gy", "gz")
LANES = 128
ROWS = 8
half = 0.5

EX, EY, EZ, PX, PY, PZ, D1, D2, D3, D4, D5, D6 = range(12)
OFFSETS = (
    (-1, 0, 0), (0, -1, 0), (0, 0, -1),
    (1, 0, 0), (0, 1, 0), (0, 0, 1),
    (1, 0, -1), (1, -1, 0), (-1, 1, 0), (0, 1, -1), (0, -1, 1), (-1, 0, 1),
)


def kernel(mesh_sizes, extent, perm, ports, amps, e_in, h_in, s_in, m_in,
           e_out, h_out, g_out,
           e_v, h_v, s_v, m_v, c_v, corr_v, src_v,
           y_e, z_e, y_p, z_p, y_h, x_h, g_v,
           r_ex, r_ey, r_ez, r_px, r_py, r_pz, r_d1, r_d2, r_d3, r_d4, r_d5, r_d6, r_g,
           in_sem, out_sem, send_sem, recv_sem, gs_sem, gr_sem):
    _, lx, ly, lz = e_in.shape
    nmat = perm.shape[0]
    nport = ports.shape[0]
    me = tuple(lax.axis_index(a) for a in AXES)
    start = (me[0] * lx, me[1] * ly, me[2] * lz)
    nz_dev = mesh_sizes[2]

    def exists(off):
        ok = None
        for a in range(3):
            if off[a] == 0:
                continue
            c = me[a] + off[a]
            t = (c >= 0) & (c < mesh_sizes[a])
            ok = t if ok is None else ok & t
        return ok

    def at(off):
        return tuple(me[a] + off[a] for a in range(3))

    loads = [
        pltpu.make_async_copy(e_in, e_v, in_sem.at[0]),
        pltpu.make_async_copy(h_in, h_v, in_sem.at[1]),
        pltpu.make_async_copy(m_in, m_v, in_sem.at[2]),
        pltpu.make_async_copy(s_in, s_v, in_sem.at[3]),
    ]
    for c in loads:
        c.start()

    barrier = pltpu.get_barrier_semaphore()
    count = jnp.int32(0)
    greet = list(OFFSETS)
    for d in range(2, nz_dev):
        greet += [(0, 0, d), (0, 0, -d)]
    for off in greet:
        ok = exists(off)
        count = count + ok.astype(jnp.int32)

        @pl.when(ok)
        def _(off=off):
            pl.semaphore_signal(barrier, inc=1, device_id=at(off), device_id_type=pl.DeviceIdType.MESH)

    recv = (r_ex, r_ey, r_ez, r_px, r_py, r_pz, r_d1, r_d2, r_d3, r_d4, r_d5, r_d6)

    def source(msg, phase):
        e = e_in if phase == 0 else e_v
        if msg == EX:
            return e.at[1:3, 0]
        if msg == EY:
            return y_e.at[phase]
        if msg == EZ:
            return z_e.at[phase]
        if msg == PX:
            return h_v.at[1:3, lx - 1]
        if msg == PY:
            return y_p.at[phase]
        if msg == PZ:
            return z_p.at[phase]
        if msg == D1:
            return e.at[0, lx - 1, :, 0:LANES]
        if msg == D2:
            return e.at[0, lx - 1, 0:ROWS, :]
        if msg == D3:
            return e.at[1, 0, ly - ROWS:ly, :]
        if msg == D4:
            return z_e.at[phase, ly - ROWS:ly, :]
        if msg == D5:
            return z_e.at[phase, 0:ROWS, :]
        return e.at[2, 0, :, lz - LANES:lz]

    def copy(msg, phase):
        return pltpu.make_async_remote_copy(
            src_ref=source(msg, phase), dst_ref=recv[msg].at[phase],
            send_sem=send_sem.at[phase, msg], recv_sem=recv_sem.at[phase, msg],
            device_id=at(OFFSETS[msg]), device_id_type=pl.DeviceIdType.MESH)

    def send(msg, phase):
        @pl.when(exists(OFFSETS[msg]))
        def _():
            copy(msg, phase).start()

    def wait_send(msg, phase):
        @pl.when(exists(OFFSETS[msg]))
        def _():
            copy(msg, phase).wait_send()

    def comes(msg):
        return exists(tuple(-o for o in OFFSETS[msg]))

    def wait_recv(msg, phase):
        @pl.when(comes(msg))
        def _():
            copy(msg, phase).wait_recv()

    for msg in range(12):
        @pl.when(jnp.logical_not(comes(msg)))
        def _(msg=msg):
            recv[msg][...] = jnp.zeros(recv[msg].shape, jnp.float32)

    row = lax.broadcasted_iota(jnp.int32, (ly, lz), 0)
    lane = lax.broadcasted_iota(jnp.int32, (ly, lz), 1)
    row1 = lax.broadcasted_iota(jnp.int32, (ly, LANES), 0)
    lane1 = lax.broadcasted_iota(jnp.int32, (ly, LANES), 1)

    def zup(v):
        return jnp.where(lane == lz - 1, 0.0, pltpu.roll(v, lz - 1, 1))

    def yup(v):
        return jnp.where(row == ly - 1, 0.0, pltpu.roll(v, ly - 1, 0))

    def pick(tile, from_lane, x, slot, acc):
        to = slot * lx + x
        shift = lax.rem(to + (LANES - from_lane), LANES)
        return jnp.where(lane1 == to, pltpu.roll(tile, shift, 1), acc)

    def place(packed, to_lane, x, slot):
        shift = lax.rem(2 * LANES + to_lane - (slot * lx + x), LANES)
        return pltpu.roll(packed, shift, 1)

    pl.semaphore_wait(barrier, count)
    for msg in (EX, D1, D2, D3, D6):
        send(msg, 0)

    plane = extent[1] * extent[2]
    port_x = []
    for p in range(nport):
        cell = ports[p]
        px = lax.div(cell, plane)
        rest = lax.rem(cell, plane)
        py = lax.div(rest, extent[2]) - start[1]
        pz = lax.rem(rest, extent[2]) - start[2]
        port_x.append(px - start[0])
        hit = (row == py) & (lane == pz)
        for s in range(STEPS):
            src_v[s, p] = jnp.where(hit, amps[s, p], 0.0)
    for s in range(STEPS):
        src_v[s, nport] = jnp.zeros((ly, lz), jnp.float32)

    loads[0].wait()

    def pack_e(x, ex, ey, ez, phase, acc):
        y_e[phase, 0, pl.ds(x, 1), :] = ex[0:1, :]
        y_e[phase, 1, pl.ds(x, 1), :] = ez[0:1, :]
        acc = pick(ex[:, 0:LANES], 0, x, 0, acc)
        acc = pick(ey[:, 0:LANES], 0, x, 1, acc)
        return pick(ez[:, lz - LANES:lz], LANES - 1, x, 2, acc)

    zero1 = jnp.zeros((ly, LANES), jnp.float32)

    def first_pack(x, acc):
        return pack_e(x, e_v[0, x], e_v[1, x], e_v[2, x], 0, acc)

    z_e[0] = lax.fori_loop(0, lx, first_pack, zero1)
    for msg in (EY, EZ, D4, D5):
        send(msg, 0)
    loads[1].wait()

    def magnetic(phase):
        def one(x, acc, last):
            ex, ey, ez = e_v[0, x], e_v[1, x], e_v[2, x]
            if last:
                dey, dez = -ey, -ez
            else:
                dey, dez = e_v[1, x + 1] - ey, e_v[2, x + 1] - ez
            hx = h_v[0, x] - half * ((yup(ez) - ez) - (zup(ey) - ey))
            hy = h_v[1, x] - half * ((zup(ex) - ex) - dez)
            hz = h_v[2, x] - half * (dey - (yup(ex) - ex))
            h_v[0, x] = hx
            h_v[1, x] = hy
            h_v[2, x] = hz
            y_p[phase, 0, pl.ds(x, 1), :] = hx[ly - 1:ly, :]
            y_p[phase, 1, pl.ds(x, 1), :] = hz[ly - 1:ly, :]
            acc = pick(hx[:, lz - LANES:lz], LANES - 1, x, 0, acc)
            return pick(hy[:, lz - LANES:lz], LANES - 1, x, 1, acc)

        acc = lax.fori_loop(0, lx - 1, lambda x, a: one(x, a, False), zero1)
        z_p[phase] = one(lx - 1, acc, True)

    flags = tuple((me[a] > 0).astype(jnp.float32) for a in range(3))

    def halos(phase):
        fx, fy, fz = flags
        d1 = pltpu.roll(r_d1[phase], LANES - 1, 1)
        d1 = jnp.concatenate([jnp.zeros((ly, lz - LANES), jnp.float32), d1], 1) if lz > LANES else d1
        x_h[0] = (r_px[phase, 0] + half * e_v[2, 0]) * fx - jnp.where(lane == lz - 1, half * d1, 0.0)
        d2 = jnp.broadcast_to(r_d2[phase, 0:1, :], (ly, lz))
        x_h[1] = (r_px[phase, 1] - half * e_v[1, 0]) * fx + jnp.where(row == ly - 1, half * d2, 0.0)
        d4 = jnp.broadcast_to(r_d4[phase, ROWS - 1:ROWS, :], (lx, LANES))
        rx = lax.broadcasted_iota(jnp.int32, (lx, LANES), 0)
        cx = lax.broadcasted_iota(jnp.int32, (lx, LANES), 1)
        d4 = jnp.sum(jnp.where(cx == rx + lx, d4, 0.0), axis=1, keepdims=True)
        ry = lax.broadcasted_iota(jnp.int32, (lx, lz), 0)
        cy = lax.broadcasted_iota(jnp.int32, (lx, lz), 1)
        y_h[0] = (r_py[phase, 0] - half * y_e[phase, 1]) * fy + jnp.where(cy == lz - 1, half * d4, 0.0)
        d3 = jnp.broadcast_to(r_d3[phase, ROWS - 1:ROWS, :], (lx, lz))
        y_h[1] = (r_py[phase, 1] + half * y_e[phase, 0]) * fy - jnp.where(ry == lx - 1, half * d3, 0.0)
        own = z_e[phase]
        fix = jnp.where(lane1 < lx, half * pltpu.roll(own, LANES - lx, 1), -half * pltpu.roll(own, lx, 1))
        zh = (r_pz[phase] + fix) * fz
        d5 = jnp.broadcast_to(pltpu.roll(r_d5[phase], LANES - 2 * lx, 1)[0:1, :], (ly, LANES))
        zh = zh - jnp.where((row1 == ly - 1) & (lane1 < lx), half * d5, 0.0)
        d6 = pltpu.roll(r_d6[phase], 2 * lx, 1)
        zh = zh + jnp.where(lane1 == 2 * lx - 1, half * d6, 0.0)
        h_v[1, lx - 1] = h_v[1, lx - 1] + half * r_ex[phase, 1]
        h_v[2, lx - 1] = h_v[2, lx - 1] - half * r_ex[phase, 0]
        return zh

    def pad_high(t):
        return jnp.concatenate([jnp.zeros((ly, lz - LANES), jnp.float32), t], 1) if lz > LANES else t

    def pad_low(t):
        return jnp.concatenate([t, jnp.zeros((ly, lz - LANES), jnp.float32)], 1) if lz > LANES else t

    def electric(step, zh):
        phase = step
        ze = r_ez[phase]

        def one(x, carry):
            hy_b, hz_b, acc = carry
            ex, ey, ez = e_v[0, x], e_v[1, x], e_v[2, x]
            top_row = row == ly - 1
            top_lane = lane == lz - 1
            eyz = pad_high(place(ze, LANES - 1, x, 1))
            exz = pad_high(place(ze, LANES - 1, x, 0))
            exy = jnp.broadcast_to(r_ey[phase, 0, pl.ds(x, 1), :], (ly, lz))
            ezy = jnp.broadcast_to(r_ey[phase, 1, pl.ds(x, 1), :], (ly, lz))
            hx = h_v[0, x] - jnp.where(top_row, half * ezy, 0.0) + jnp.where(top_lane, half * eyz, 0.0)
            hy = h_v[1, x] - jnp.where(top_lane, half * exz, 0.0)
            hz = h_v[2, x] + jnp.where(top_row, half * exy, 0.0)
            h_v[0, x] = hx
            h_v[1, x] = hy
            h_v[2, x] = hz
            low_row = row == 0
            low_lane = lane == 0
            hx_y = jnp.where(low_row, jnp.broadcast_to(y_h[0, pl.ds(x, 1), :], (ly, lz)), pltpu.roll(hx, 1, 0))
            hz_y = jnp.where(low_row, jnp.broadcast_to(y_h[1, pl.ds(x, 1), :], (ly, lz)), pltpu.roll(hz, 1, 0))
            hx_z = jnp.where(low_lane, pad_low(place(zh, 0, x, 0)), pltpu.roll(hx, 1, 1))
            hy_z = jnp.where(low_lane, pad_low(place(zh, 0, x, 1)), pltpu.roll(hy, 1, 1))
            c = c_v[x]
            ex = ex + c * ((hz - hz_y) - (hy - hy_z))
            ey = ey + c * ((hx - hx_z) - (hz - hz_b))
            ez = ez + c * ((hy - hy_b) - (hx - hx_y))
            for p in range(nport):
                ez = ez + src_v[step, jnp.where(port_x[p] == x, p, nport)]
            e_v[0, x] = ex
            e_v[1, x] = ey
            e_v[2, x] = ez
            total = None
            for comp, val in enumerate((ex, ey, ez)):
                change = s_v[step, comp, x].astype(jnp.float32) - s_v[step + 1, comp, x].astype(jnp.float32)
                t = val * change
                total = t if total is None else total + t
            fold = total[:, 0:LANES]
            for k in range(1, lz // LANES):
                fold = fold + total[:, k * LANES:(k + 1) * LANES]
            if step == 0:
                corr_v[x] = fold
            else:
                fold = fold + corr_v[x]
            if step + 1 < STEPS:
                acc = pack_e(x, ex, ey, ez, phase + 1, acc)
            else:
                acc = jnp.where(lane1 == x, jnp.sum(fold, axis=1, keepdims=True), acc)
            return hy, hz, acc

        _, _, acc = lax.fori_loop(0, lx, one, (x_h[0], x_h[1], zero1))
        return acc

    magnetic(0)
    for msg in (PX, PY, PZ):
        send(msg, 0)

    loads[2].wait()
    coefs = [half / jnp.full((ly, lz), perm[k], jnp.float32) for k in range(nmat)]

    def coef_plane(x, carry):
        mat = m_v[x]
        c = coefs[0]
        for k in range(1, nmat):
            c = jnp.where(mat == k, coefs[k], c)
        c_v[x] = c
        return carry

    lax.fori_loop(0, lx, coef_plane, 0)
    loads[3].wait()

    for step in range(STEPS):
        if step > 0:
            for msg in (EX, D1, D2, D3, D6, EY, EZ, D4, D5):
                send(msg, step)
            magnetic(step)
            for msg in (PX, PY, PZ):
                send(msg, step)
        for msg in range(12):
            wait_send(msg, step)
        for msg in range(12):
            wait_recv(msg, step)
        zh = halos(step)
        acc = electric(step, zh)
        if step + 1 < STEPS:
            z_e[step + 1] = acc

    outs = [
        pltpu.make_async_copy(e_v, e_out, out_sem.at[0]),
        pltpu.make_async_copy(h_v, h_out, out_sem.at[1]),
    ]
    for c in outs:
        c.start()

    own_rows = ly // nz_dev
    g_v[...] = acc

    def tile_of(k):
        return pl.ds(pl.multiple_of((k * own_rows) // ROWS * ROWS, ROWS), ROWS)

    gcopies = []
    for d in range(1, nz_dev):
        peer = lax.rem(me[2] + d, nz_dev)
        gcopies.append(pltpu.make_async_remote_copy(
            src_ref=g_v.at[tile_of(peer)], dst_ref=r_g.at[d - 1],
            send_sem=gs_sem.at[d - 1], recv_sem=gr_sem.at[d - 1],
            device_id=(me[0], me[1], peer), device_id_type=pl.DeviceIdType.MESH))
    for c in gcopies:
        c.start()
    total = g_v[tile_of(me[2])]
    for d, c in enumerate(gcopies):
        c.wait_recv()
        total = total + r_g[d]
    shift = lax.rem(ROWS - lax.rem(me[2] * own_rows, ROWS), ROWS)
    g_out[...] = pltpu.roll(total, shift, 0)
    for c in gcopies:
        c.wait_send()
    for c in outs:
        c.wait()


def solution(mesh):
    mesh_sizes = tuple(mesh.shape[a] for a in AXES)

    def body(e_adjoint, h_adjoint, snapshots, material, permittivity, design_mask, ports, amplitudes):
        _, lx, ly, lz = e_adjoint.shape
        extent = (lx * mesh_sizes[0], ly * mesh_sizes[1], lz * mesh_sizes[2])
        nport = ports.shape[0]
        f32 = jnp.float32
        any_spec = pl.BlockSpec(memory_space=pl.ANY)
        smem = pl.BlockSpec(memory_space=pltpu.SMEM)
        e, h, g = pl.pallas_call(
            lambda *refs: kernel(mesh_sizes, extent, *refs),
            out_shape=(
                jax.ShapeDtypeStruct(e_adjoint.shape, f32),
                jax.ShapeDtypeStruct(h_adjoint.shape, f32),
                jax.ShapeDtypeStruct((ROWS, LANES), f32),
            ),
            in_specs=[smem, smem, smem, any_spec, any_spec, any_spec, any_spec],
            out_specs=(any_spec, any_spec, pl.BlockSpec(memory_space=pltpu.VMEM)),
            scratch_shapes=[
                pltpu.VMEM((3, lx, ly, lz), f32),
                pltpu.VMEM((3, lx, ly, lz), f32),
                pltpu.VMEM(snapshots.shape, snapshots.dtype),
                pltpu.VMEM((lx, ly, lz), jnp.int32),
                pltpu.VMEM((lx, ly, lz), f32),
                pltpu.VMEM((lx, ly, LANES), f32),
                pltpu.VMEM((STEPS, nport + 1, ly, lz), f32),
                pltpu.VMEM((STEPS, 2, lx, lz), f32),
                pltpu.VMEM((STEPS, ly, LANES), f32),
                pltpu.VMEM((STEPS, 2, lx, lz), f32),
                pltpu.VMEM((STEPS, ly, LANES), f32),
                pltpu.VMEM((2, lx, lz), f32),
                pltpu.VMEM((2, ly, lz), f32),
                pltpu.VMEM((ly, LANES), f32),
                pltpu.VMEM((STEPS, 2, ly, lz), f32),
                pltpu.VMEM((STEPS, 2, lx, lz), f32),
                pltpu.VMEM((STEPS, ly, LANES), f32),
                pltpu.VMEM((STEPS, 2, ly, lz), f32),
                pltpu.VMEM((STEPS, 2, lx, lz), f32),
                pltpu.VMEM((STEPS, ly, LANES), f32),
                pltpu.VMEM((STEPS, ly, LANES), f32),
                pltpu.VMEM((STEPS, ROWS, lz), f32),
                pltpu.VMEM((STEPS, ROWS, lz), f32),
                pltpu.VMEM((STEPS, ROWS, LANES), f32),
                pltpu.VMEM((STEPS, ROWS, LANES), f32),
                pltpu.VMEM((STEPS, ly, LANES), f32),
                pltpu.VMEM((3, ROWS, LANES), f32),
                pltpu.SemaphoreType.DMA((4,)),
                pltpu.SemaphoreType.DMA((2,)),
                pltpu.SemaphoreType.DMA((STEPS, 12)),
                pltpu.SemaphoreType.DMA((STEPS, 12)),
                pltpu.SemaphoreType.DMA((3,)),
                pltpu.SemaphoreType.DMA((3,)),
            ],
            compiler_params=pltpu.CompilerParams(collective_id=0, has_side_effects=True),
            name="reverse_steps",
        )(permittivity, ports, amplitudes, e_adjoint, h_adjoint, snapshots, material)
        own = ly // mesh_sizes[2]
        mask = lax.dynamic_slice_in_dim(design_mask, lax.axis_index("gz") * own, own, 1)
        gradient = mask.astype(f32) * g[:own, :lx].T
        return e, h, gradient

    placed = (
        P(None, "gx", "gy", "gz"),
        P(None, "gx", "gy", "gz"),
        P(None, None, "gx", "gy", "gz"),
        P("gx", "gy", "gz"),
        P(),
        P("gx", "gy"),
        P(),
        P(),
    )
    return jax.shard_map(
        body,
        mesh=mesh,
        in_specs=placed,
        out_specs=(P(None, "gx", "gy", "gz"), P(None, "gx", "gy", "gz"), P("gx", ("gy", "gz"))),
        check_vma=False,
    )
```

time: 140 us -> 51.5 us (0.37); the launches traced: 138 us -> 51.3 us
  Pallas kernels: 0 us -> 45.4 us
  local copies, waits for them, and re-layouts: 39.9 us -> 3.93 us
  starting transfers between devices: 30.9 us -> 0 us
  other arithmetic: 28.5 us -> 1.28 us
  waiting for transfers between devices: 21.5 us -> 0 us
  blocking collectives: 9.59 us -> 0 us
  between operations: 7.9 us -> 0.65 us
    pallas_call x0 -> x1, Pallas kernels: none -> 45.4 us  [body(): pl.pallas_call(lambda *refs: kernel(mesh_sizes, extent, *refs), out_shape...]
    ppermute x12 -> x0, starting transfers between devices: 30.9 us -> none  [from_behind(): return lax.ppermute(array, axis, pairs)]
    ppermute x12 -> x0, waiting for transfers between devices: 21.5 us -> none  [from_behind(): return lax.ppermute(array, axis, pairs)]
    slice x21 -> x0, local copies, waits for them, and re-layouts: 15.2 us -> none  [the longest x1 2.6 us: split_step(): magnetic[2] - magnetic_step * (ey_xp - electric[1] - (ex_yp - electric[0]))]
    squeeze x34 -> x0, local copies, waits for them, and re-layouts: 11.1 us -> none  [the longest x3 3 us: split_step(): ey_zp = jnp.concatenate([electric[1, :, :, 1:], from_z[1]], 2)]
    unnamed x1 -> x0, blocking collectives: 9.59 us -> none
    unnamed x104 -> x4, local copies, waits for them, and re-layouts: 12.3 us -> 3.93 us
    add x3 -> x0, other arithmetic: 7.64 us -> none  [the longest x1 3.1 us: split_step(): electric[2] + coef * (magnetic[1] - hy_xm - (magnetic[0] - hx_ym)) + source]
  transfers between devices with their start and end apart: 12 -> 0, of which waited for: 5 -> 0; matrix products, arithmetic and copies ran while one was open for 29% -> 0% of each run, Pallas kernels for 0% -> 0%
where the time goes in v1:
time: 51.5 us; the launch traced here: 51.3 us
  Pallas kernels  45.4 us (88%)
  local copies, waits for them, and re-layouts  3.93 us (8%)
  other arithmetic  1.28 us (2%)
  between operations  0.65 us (1%)
    pallas_call x1, Pallas kernels, body(): pl.pallas_call(lambda *refs: kernel(mesh_sizes, extent, *refs), out_shape...  45.4 us
    unnamed x4, local copies, waits for them, and re-layouts  3.93 us
    mul x1, other arithmetic, body(): gradient = mask.astype(f32) * g[:own, :lx].T  1.28 us

profile of v1, /device:TPU:160, one launch (start us, length us, event | category | flops | bytes accessed | tf_op | source)
XLA Modules:
  0.0 51.3 jit_solution(17876972615323116283)
XLA Ops:
  0.6 45.4 %reverse_steps.1 = (f32[3,32,16,256]{3,2,1,0:T(8,128)}, f32[3,32,16,256]{3,2,1,0:T(8,128)}, f32[8,128]{1,0:T(8,128)}) custom-call(f32[8]{0:T(128)} %refs_0_.1, s32[3]{0:T(128)} %refs_1_.1, f32[2,3]{1,0:T(2,128)} %refs_2_.1, f32[3,32,16,256]{3,2,1,0:T(8,128)} %refs_3_.1, f32[3,32,16,256]{3,2,1,0:T(8,128)} %refs_4_.1, bf16[3,3,32,16,256]{4,3,2,1,0:T(8,128)(2,1)} %refs_5_.1, ...), custom_call_target="tpu_custom_call" | custom-call | tf_op jit(solution)/shard_map/reverse_steps/pallas_call | solution.py:374
  46.1 1.3 %bitcast_multiply_fusion = f32[32,4]{0,1:T(4,128)} fusion(f32[8,128]{1,0:T(8,128)} %get-tuple-element.8, s32[32,16]{0,1:T(8,128)} %param.13, s32[]{:T(128)S(6)} %select_n.3), kind=kLoop, calls=%fused_computation | loop fusion | flops 256 | bytes 1540 | tf_op jit(solution)/shard_map/mul | solution.py:423
  47.4 0.0 copy-start
  47.4 2.8 %copy.13 = f32[3,32,16,256]{3,2,1,0:T(8,128)} copy(f32[3,32,16,256]{3,2,1,0:T(8,128)} %get-tuple-element.12) | data formatting | bytes 3145728
  50.1 0.0 copy-done
  50.2 1.1 %copy.14 = f32[3,32,16,256]{3,2,1,0:T(8,128)} copy(f32[3,32,16,256]{3,2,1,0:T(8,128)S(1)} %copy-done) | data formatting | bytes 3145728
Async XLA Ops:
  47.4 2.8 %copy-start = (f32[3,32,16,256]{3,2,1,0:T(8,128)S(1)}, f32[3,32,16,256]{3,2,1,0:T(8,128)}, u32[]{:S(2)}) copy-start(f32[3,32,16,256]{3,2,1,0:T(8,128)} %get-tuple-element.13) | copy-start | bytes 4718596

commit v2 on v1

--- a/solution.py
+++ b/solution.py
@@ -10,6 +10,7 @@
 LANES = 128
 ROWS = 8
 half = 0.5
+UP, UM, UE = 8, 8, 8
 
 EX, EY, EZ, PX, PY, PZ, D1, D2, D3, D4, D5, D6 = range(12)
 OFFSETS = (
@@ -46,7 +47,7 @@
         return tuple(me[a] + off[a] for a in range(3))
 
     loads = [
-        pltpu.make_async_copy(e_in, e_v, in_sem.at[0]),
+        pltpu.make_async_copy(e_in, e_v.at[:, 0:lx], in_sem.at[0]),
         pltpu.make_async_copy(h_in, h_v, in_sem.at[1]),
         pltpu.make_async_copy(m_in, m_v, in_sem.at[2]),
         pltpu.make_async_copy(s_in, s_v, in_sem.at[3]),
@@ -119,6 +120,9 @@
         def _():
             copy(msg, phase).wait_recv()
 
+    for c in (1, 2):
+        e_v[c, lx] = jnp.zeros((ly, lz), jnp.float32)
+
     for msg in range(12):
         @pl.when(jnp.logical_not(comes(msg)))
         def _(msg=msg):
@@ -177,18 +181,15 @@
     def first_pack(x, acc):
         return pack_e(x, e_v[0, x], e_v[1, x], e_v[2, x], 0, acc)
 
-    z_e[0] = lax.fori_loop(0, lx, first_pack, zero1)
+    z_e[0] = lax.fori_loop(0, lx, first_pack, zero1, unroll=UP)
     for msg in (EY, EZ, D4, D5):
         send(msg, 0)
     loads[1].wait()
 
     def magnetic(phase):
-        def one(x, acc, last):
+        def one(x, acc):
             ex, ey, ez = e_v[0, x], e_v[1, x], e_v[2, x]
-            if last:
-                dey, dez = -ey, -ez
-            else:
-                dey, dez = e_v[1, x + 1] - ey, e_v[2, x + 1] - ez
+            dey, dez = e_v[1, x + 1] - ey, e_v[2, x + 1] - ez
             hx = h_v[0, x] - half * ((yup(ez) - ez) - (zup(ey) - ey))
             hy = h_v[1, x] - half * ((zup(ex) - ex) - dez)
             hz = h_v[2, x] - half * (dey - (yup(ex) - ex))
@@ -200,8 +201,7 @@
             acc = pick(hx[:, lz - LANES:lz], LANES - 1, x, 0, acc)
             return pick(hy[:, lz - LANES:lz], LANES - 1, x, 1, acc)
 
-        acc = lax.fori_loop(0, lx - 1, lambda x, a: one(x, a, False), zero1)
-        z_p[phase] = one(lx - 1, acc, True)
+        z_p[phase] = lax.fori_loop(0, lx, one, zero1, unroll=UM)
 
     flags = tuple((me[a] > 0).astype(jnp.float32) for a in range(3))
 
@@ -290,7 +290,7 @@
                 acc = jnp.where(lane1 == x, jnp.sum(fold, axis=1, keepdims=True), acc)
             return hy, hz, acc
 
-        _, _, acc = lax.fori_loop(0, lx, one, (x_h[0], x_h[1], zero1))
+        _, _, acc = lax.fori_loop(0, lx, one, (x_h[0], x_h[1], zero1), unroll=UE)
         return acc
 
     magnetic(0)
@@ -308,7 +308,7 @@
         c_v[x] = c
         return carry
 
-    lax.fori_loop(0, lx, coef_plane, 0)
+    lax.fori_loop(0, lx, coef_plane, 0, unroll=UP)
     loads[3].wait()
 
     for step in range(STEPS):
@@ -328,17 +328,18 @@
             z_e[step + 1] = acc
 
     outs = [
-        pltpu.make_async_copy(e_v, e_out, out_sem.at[0]),
+        pltpu.make_async_copy(e_v.at[:, 0:lx], e_out, out_sem.at[0]),
         pltpu.make_async_copy(h_v, h_out, out_sem.at[1]),
     ]
     for c in outs:
         c.start()
 
     own_rows = ly // nz_dev
+    tile = g_out.shape[0]
     g_v[...] = acc
 
     def tile_of(k):
-        return pl.ds(pl.multiple_of((k * own_rows) // ROWS * ROWS, ROWS), ROWS)
+        return pl.ds(pl.multiple_of((k * own_rows) // tile * tile, ROWS), tile)
 
     gcopies = []
     for d in range(1, nz_dev):
@@ -353,7 +354,7 @@
     for d, c in enumerate(gcopies):
         c.wait_recv()
         total = total + r_g[d]
-    shift = lax.rem(ROWS - lax.rem(me[2] * own_rows, ROWS), ROWS)
+    shift = lax.rem(tile - lax.rem(me[2] * own_rows, tile), tile)
     g_out[...] = pltpu.roll(total, shift, 0)
     for c in gcopies:
         c.wait_send()
@@ -369,6 +370,8 @@
         extent = (lx * mesh_sizes[0], ly * mesh_sizes[1], lz * mesh_sizes[2])
         nport = ports.shape[0]
         f32 = jnp.float32
+        own = ly // mesh_sizes[2]
+        tile = max(ROWS, own)
         any_spec = pl.BlockSpec(memory_space=pl.ANY)
         smem = pl.BlockSpec(memory_space=pltpu.SMEM)
         e, h, g = pl.pallas_call(
@@ -376,12 +379,12 @@
             out_shape=(
                 jax.ShapeDtypeStruct(e_adjoint.shape, f32),
                 jax.ShapeDtypeStruct(h_adjoint.shape, f32),
-                jax.ShapeDtypeStruct((ROWS, LANES), f32),
+                jax.ShapeDtypeStruct((tile, LANES), f32),
             ),
             in_specs=[smem, smem, smem, any_spec, any_spec, any_spec, any_spec],
             out_specs=(any_spec, any_spec, pl.BlockSpec(memory_space=pltpu.VMEM)),
             scratch_shapes=[
-                pltpu.VMEM((3, lx, ly, lz), f32),
+                pltpu.VMEM((3, lx + 1, ly, lz), f32),
                 pltpu.VMEM((3, lx, ly, lz), f32),
                 pltpu.VMEM(snapshots.shape, snapshots.dtype),
                 pltpu.VMEM((lx, ly, lz), jnp.int32),
@@ -407,7 +410,7 @@
                 pltpu.VMEM((STEPS, ROWS, LANES), f32),
                 pltpu.VMEM((STEPS, ROWS, LANES), f32),
                 pltpu.VMEM((STEPS, ly, LANES), f32),
-                pltpu.VMEM((3, ROWS, LANES), f32),
+                pltpu.VMEM((3, tile, LANES), f32),
                 pltpu.SemaphoreType.DMA((4,)),
                 pltpu.SemaphoreType.DMA((2,)),
                 pltpu.SemaphoreType.DMA((STEPS, 12)),
@@ -418,7 +421,6 @@
             compiler_params=pltpu.CompilerParams(collective_id=0, has_side_effects=True),
             name="reverse_steps",
         )(permittivity, ports, amplitudes, e_adjoint, h_adjoint, snapshots, material)
-        own = ly // mesh_sizes[2]
         mask = lax.dynamic_slice_in_dim(design_mask, lax.axis_index("gz") * own, own, 1)
         gradient = mask.astype(f32) * g[:own, :lx].T
         return e, h, gradient

time: 51.5 us -> 31.9 us (0.62)
  Pallas kernels: 45.4 us -> 25.8 us
    pallas_call x1, Pallas kernels: 45.4 us -> 25.8 us  [body(): pl.pallas_call(lambda *refs: kernel(mesh_sizes, extent, *refs), out_shape...]
where the time goes in v2:
time: 31.9 us; the launch traced here: 31.7 us
  Pallas kernels  25.8 us (81%)
  local copies, waits for them, and re-layouts  3.93 us (12%)
  other arithmetic  1.28 us (4%)
  between operations  0.65 us (2%)
    pallas_call x1, Pallas kernels, body(): pl.pallas_call(lambda *refs: kernel(mesh_sizes, extent, *refs), out_shape...  25.8 us
    unnamed x4, local copies, waits for them, and re-layouts  3.93 us
    mul x1, other arithmetic, body(): gradient = mask.astype(f32) * g[:own, :lx].T  1.28 us

profile of v2, /device:TPU:160, one launch (start us, length us, event | category | flops | bytes accessed | tf_op | source)
XLA Modules:
  0.0 31.7 jit_solution(17515153526099787698)
XLA Ops:
  0.6 25.8 %reverse_steps.1 = (f32[3,32,16,256]{3,2,1,0:T(8,128)}, f32[3,32,16,256]{3,2,1,0:T(8,128)}, f32[8,128]{1,0:T(8,128)}) custom-call(f32[8]{0:T(128)} %refs_0_.1, s32[3]{0:T(128)} %refs_1_.1, f32[2,3]{1,0:T(2,128)} %refs_2_.1, f32[3,32,16,256]{3,2,1,0:T(8,128)} %refs_3_.1, f32[3,32,16,256]{3,2,1,0:T(8,128)} %refs_4_.1, bf16[3,3,32,16,256]{4,3,2,1,0:T(8,128)(2,1)} %refs_5_.1, ...), custom_call_target="tpu_custom_call" | custom-call | tf_op jit(solution)/shard_map/reverse_steps/pallas_call | solution.py:377
  26.5 1.3 %bitcast_multiply_fusion = f32[32,4]{0,1:T(4,128)} fusion(f32[8,128]{1,0:T(8,128)} %get-tuple-element.8, s32[32,16]{0,1:T(8,128)} %param.13, s32[]{:T(128)S(6)} %select_n.3), kind=kLoop, calls=%fused_computation | loop fusion | flops 256 | bytes 1540 | tf_op jit(solution)/shard_map/mul | solution.py:425
  27.8 0.0 copy-start
  27.8 2.8 %copy.13 = f32[3,32,16,256]{3,2,1,0:T(8,128)} copy(f32[3,32,16,256]{3,2,1,0:T(8,128)} %get-tuple-element.12) | data formatting | bytes 3145728
  30.5 0.0 copy-done
  30.5 1.1 %copy.14 = f32[3,32,16,256]{3,2,1,0:T(8,128)} copy(f32[3,32,16,256]{3,2,1,0:T(8,128)S(1)} %copy-done) | data formatting | bytes 3145728
Async XLA Ops:
  27.8 2.8 %copy-start = (f32[3,32,16,256]{3,2,1,0:T(8,128)S(1)}, f32[3,32,16,256]{3,2,1,0:T(8,128)}, u32[]{:S(2)}) copy-start(f32[3,32,16,256]{3,2,1,0:T(8,128)} %get-tuple-element.13) | copy-start | bytes 4718596

commit v3 on v2

--- a/solution.py
+++ b/solution.py
@@ -20,12 +20,12 @@
 )
 
 
-def kernel(mesh_sizes, extent, perm, ports, amps, e_in, h_in, s_in, m_in,
-           e_out, h_out, g_out,
-           e_v, h_v, s_v, m_v, c_v, corr_v, src_v,
+def kernel(mesh_sizes, extent, perm, ports, amps, mask, e_in, h_in, s_in, m_in,
+           e_v, h_v, g_out,
+           s_v, m_v, c_v, corr_v, src_v,
            y_e, z_e, y_p, z_p, y_h, x_h, g_v,
            r_ex, r_ey, r_ez, r_px, r_py, r_pz, r_d1, r_d2, r_d3, r_d4, r_d5, r_d6, r_g,
-           in_sem, out_sem, send_sem, recv_sem, gs_sem, gr_sem):
+           in_sem, send_sem, recv_sem, gs_sem, gr_sem):
     _, lx, ly, lz = e_in.shape
     nmat = perm.shape[0]
     nport = ports.shape[0]
@@ -327,16 +327,10 @@
         if step + 1 < STEPS:
             z_e[step + 1] = acc
 
-    outs = [
-        pltpu.make_async_copy(e_v.at[:, 0:lx], e_out, out_sem.at[0]),
-        pltpu.make_async_copy(h_v, h_out, out_sem.at[1]),
-    ]
-    for c in outs:
-        c.start()
-
     own_rows = ly // nz_dev
     tile = g_out.shape[0]
     g_v[...] = acc
+    g_v[:, 0:lx] = acc[:, 0:lx] * mask[...].astype(jnp.float32)
 
     def tile_of(k):
         return pl.ds(pl.multiple_of((k * own_rows) // tile * tile, ROWS), tile)
@@ -358,6 +352,17 @@
     g_out[...] = pltpu.roll(total, shift, 0)
     for c in gcopies:
         c.wait_send()
+
+
+def write_out(e_v, h_v, g_v, e_out, h_out, g_out, sem):
+    lx = h_v.shape[1]
+    outs = [
+        pltpu.make_async_copy(e_v.at[:, 0:lx], e_out, sem.at[0]),
+        pltpu.make_async_copy(h_v, h_out, sem.at[1]),
+    ]
+    for c in outs:
+        c.start()
+    g_out[...] = g_v[0:g_out.shape[0], 0:g_out.shape[1]]
     for c in outs:
         c.wait()
 
@@ -374,18 +379,17 @@
         tile = max(ROWS, own)
         any_spec = pl.BlockSpec(memory_space=pl.ANY)
         smem = pl.BlockSpec(memory_space=pltpu.SMEM)
+        vmem = pl.BlockSpec(memory_space=pltpu.VMEM)
         e, h, g = pl.pallas_call(
             lambda *refs: kernel(mesh_sizes, extent, *refs),
             out_shape=(
-                jax.ShapeDtypeStruct(e_adjoint.shape, f32),
-                jax.ShapeDtypeStruct(h_adjoint.shape, f32),
-                jax.ShapeDtypeStruct((tile, LANES), f32),
-            ),
-            in_specs=[smem, smem, smem, any_spec, any_spec, any_spec, any_spec],
-            out_specs=(any_spec, any_spec, pl.BlockSpec(memory_space=pltpu.VMEM)),
-            scratch_shapes=[
                 pltpu.VMEM((3, lx + 1, ly, lz), f32),
                 pltpu.VMEM((3, lx, ly, lz), f32),
+                pltpu.VMEM((tile, LANES), f32),
+            ),
+            in_specs=[smem, smem, smem, vmem, any_spec, any_spec, any_spec, any_spec],
+            out_specs=(vmem, vmem, vmem),
+            scratch_shapes=[
                 pltpu.VMEM(snapshots.shape, snapshots.dtype),
                 pltpu.VMEM((lx, ly, lz), jnp.int32),
                 pltpu.VMEM((lx, ly, lz), f32),
@@ -412,7 +416,6 @@
                 pltpu.VMEM((STEPS, ly, LANES), f32),
                 pltpu.VMEM((3, tile, LANES), f32),
                 pltpu.SemaphoreType.DMA((4,)),
-                pltpu.SemaphoreType.DMA((2,)),
                 pltpu.SemaphoreType.DMA((STEPS, 12)),
                 pltpu.SemaphoreType.DMA((STEPS, 12)),
                 pltpu.SemaphoreType.DMA((3,)),
@@ -420,10 +423,21 @@
             ],
             compiler_params=pltpu.CompilerParams(collective_id=0, has_side_effects=True),
             name="reverse_steps",
-        )(permittivity, ports, amplitudes, e_adjoint, h_adjoint, snapshots, material)
-        mask = lax.dynamic_slice_in_dim(design_mask, lax.axis_index("gz") * own, own, 1)
-        gradient = mask.astype(f32) * g[:own, :lx].T
-        return e, h, gradient
+        )(permittivity, ports, amplitudes, design_mask.T, e_adjoint, h_adjoint, snapshots, material)
+        e, h, g = (pltpu.with_memory_space_constraint(v, pltpu.VMEM) for v in (e, h, g))
+        e, h, g = pl.pallas_call(
+            write_out,
+            out_shape=(
+                jax.ShapeDtypeStruct(e_adjoint.shape, f32),
+                jax.ShapeDtypeStruct(h_adjoint.shape, f32),
+                jax.ShapeDtypeStruct((own, lx), f32),
+            ),
+            in_specs=[vmem, vmem, vmem],
+            out_specs=(any_spec, any_spec, vmem),
+            scratch_shapes=[pltpu.SemaphoreType.DMA((2,))],
+            name="write_out",
+        )(e, h, g)
+        return e, h, g.T
 
     placed = (
         P(None, "gx", "gy", "gz"),

time: 31.9 us -> 28.3 us (0.89)
  local copies, waits for them, and re-layouts: 3.93 us -> 0 us
  Pallas kernels: 25.8 us -> 27.5 us
  other arithmetic: 1.28 us -> 0 us
    unnamed x4 -> x0, local copies, waits for them, and re-layouts: 3.93 us -> none
    pallas_call x0 -> x1, Pallas kernels: none -> 2.26 us  [body(): pl.pallas_call(write_out, out_shape=(jax.ShapeDtypeStruct(e_adjoint.shape...]
    mul x1 -> x0, other arithmetic: 1.28 us -> none  [body(): gradient = mask.astype(f32) * g[:own, :lx].T]
    pallas_call x1, Pallas kernels: 25.8 us -> 25.2 us  [body(): pl.pallas_call(lambda *refs: kernel(mesh_sizes, extent, *refs), out_shape...]
where the time goes in v3:
time: 28.3 us; the launch traced here: 28.1 us
  Pallas kernels  27.5 us (97%)
  between operations  0.64 us (2%)
    pallas_call x1, Pallas kernels, body(): pl.pallas_call(lambda *refs: kernel(mesh_sizes, extent, *refs), out_shape...  25.2 us
    pallas_call x1, Pallas kernels, body(): pl.pallas_call(write_out, out_shape=(jax.ShapeDtypeStruct(e_adjoint.shape...  2.26 us

profile of v3, /device:TPU:160, one launch (start us, length us, event | category | flops | bytes accessed | tf_op | source)
XLA Modules:
  0.0 28.1 jit_solution(5827908659507322786)
XLA Ops:
  0.6 25.2 %reverse_steps.1 = (f32[3,33,16,256]{3,2,1,0:T(8,128)S(1)}, f32[3,32,16,256]{3,2,1,0:T(8,128)S(1)}, f32[8,128]{1,0:T(8,128)S(1)}) custom-call(f32[8]{0:T(128)} %refs_0_.1, s32[3]{0:T(128)} %refs_1_.1, f32[2,3]{1,0:T(2,128)} %refs_2_.1, s32[16,32]{1,0:T(8,128)} %bitcast.2, f32[3,32,16,256]{3,2,1,0:T(8,128)} %refs_4_.1, f32[3,32,16,256]{3,2,1,0:T(8,128)} %refs_5_.1, ...), custom_call_target="tpu_custom_call" | custom-call | tf_op jit(solution)/shard_map/reverse_steps/pallas_call | solution.py:383
  25.9 2.3 %write_out.1 = (f32[3,32,16,256]{3,2,1,0:T(8,128)}, f32[3,32,16,256]{3,2,1,0:T(8,128)}, f32[4,32]{1,0:T(4,128)}) custom-call(f32[3,33,16,256]{3,2,1,0:T(8,128)S(1)} %get-tuple-element.9.e_v, f32[3,32,16,256]{3,2,1,0:T(8,128)S(1)} %get-tuple-element.10.h_v, f32[8,128]{1,0:T(8,128)S(1)} %get-tuple-element.11.g_v), custom_call_target="tpu_custom_call" | custom-call | tf_op jit(solution)/shard_map/write_out/pallas_call | solution.py:428

commit v4 on v3

v4 whole, which is shorter than its diff:
```python
import jax
import jax.numpy as jnp
from jax import lax
from jax.experimental import pallas as pl
from jax.experimental.pallas import tpu as pltpu
from jax.sharding import PartitionSpec as P

STEPS = 2
AXES = ("gx", "gy", "gz")
LANES = 128
ROWS = 8
half = 0.5
U_MAG, U_PRE, U_POST = 8, 8, 8
CHUNKS = 4

EX, EY, EZ, PX, PY, PZ, D1, D2, D3, D4, D5, D6 = range(12)
OFFSETS = (
    (-1, 0, 0), (0, -1, 0), (0, 0, -1),
    (1, 0, 0), (0, 1, 0), (0, 0, 1),
    (1, 0, -1), (1, -1, 0), (-1, 1, 0), (0, 1, -1), (0, -1, 1), (-1, 0, 1),
)


def kernel(mesh_sizes, extent, perm, ports, amps, mask, e_in, h_in, s_in, m_in,
           e_v, h_v, g_out,
           s_v, m_v, c_v, corr_v, diff_v, src_v,
           x_e, y_e, z_e, x_p, y_p, z_p, y_t, rows_v, g_v,
           r_ex, r_ey, r_ez, r_px, r_py, r_pz, r_d1, r_d2, r_d3, r_d4, r_d5, r_d6, r_g,
           in_sem, send_sem, recv_sem, gs_sem, gr_sem):
    _, lx, ly, lz = e_in.shape
    nt = lz // LANES
    off = 2 * lx
    f32 = jnp.float32
    nmat = perm.shape[0]
    nport = ports.shape[0]
    me = tuple(lax.axis_index(a) for a in AXES)
    start = (me[0] * lx, me[1] * ly, me[2] * lz)
    nz_dev = mesh_sizes[2]

    def exists(o):
        ok = None
        for a in range(3):
            if o[a] == 0:
                continue
            c = me[a] + o[a]
            t = (c >= 0) & (c < mesh_sizes[a])
            ok = t if ok is None else ok & t
        return ok

    def at(o):
        return tuple(me[a] + o[a] for a in range(3))

    step_x = lx // CHUNKS
    load_e, load_h = [], []
    for k in range(CHUNKS):
        d = pl.ds(k * step_x, step_x)
        load_e.append(pltpu.make_async_copy(e_in.at[:, d], e_v.at[:, d], in_sem.at[2 + k]))
        load_h.append(pltpu.make_async_copy(h_in.at[:, d], h_v.at[:, d], in_sem.at[2 + CHUNKS + k]))
    load_m = pltpu.make_async_copy(m_in, m_v, in_sem.at[0])
    load_s = pltpu.make_async_copy(s_in, s_v, in_sem.at[1])
    for c in load_e + load_h + [load_m, load_s]:
        c.start()

    barrier = pltpu.get_barrier_semaphore()
    count = jnp.int32(0)
    greet = list(OFFSETS)
    for d in range(2, nz_dev):
        greet += [(0, 0, d), (0, 0, -d)]
    for o in greet:
        ok = exists(o)
        count = count + ok.astype(jnp.int32)

        @pl.when(ok)
        def _(o=o):
            pl.semaphore_signal(barrier, inc=1, device_id=at(o), device_id_type=pl.DeviceIdType.MESH)

    recv = (r_ex, r_ey, r_ez, r_px, r_py, r_pz, r_d1, r_d2, r_d3, r_d4, r_d5, r_d6)

    def source(msg, phase):
        first = phase == 0
        if msg == EX:
            return e_in.at[1:3, 0] if first else x_e.at[phase, 0:2]
        if msg == EY:
            return y_e.at[phase]
        if msg == EZ:
            return z_e.at[phase]
        if msg == PX:
            return x_p.at[phase]
        if msg == PY:
            return y_p.at[phase]
        if msg == PZ:
            return z_p.at[phase]
        if msg == D1:
            return e_in.at[0, lx - 1, :, 0:LANES] if first else x_e.at[phase, 2, :, 0:LANES]
        if msg == D2:
            return e_in.at[0, lx - 1, 0:ROWS, :] if first else x_e.at[phase, 2, 0:ROWS, :]
        if msg == D3:
            return e_in.at[1, 0, ly - ROWS:ly, :] if first else x_e.at[phase, 0, ly - ROWS:ly, :]
        if msg == D4:
            return z_e.at[phase, ly - ROWS:ly, :]
        if msg == D5:
            return z_e.at[phase, 0:ROWS, :]
        return e_in.at[2, 0, :, lz - LANES:lz] if first else x_e.at[phase, 1, :, lz - LANES:lz]

    def copy(msg, phase):
        return pltpu.make_async_remote_copy(
            src_ref=source(msg, phase), dst_ref=recv[msg].at[phase],
            send_sem=send_sem.at[phase, msg], recv_sem=recv_sem.at[phase, msg],
            device_id=at(OFFSETS[msg]), device_id_type=pl.DeviceIdType.MESH)

    def send(msg, phase):
        @pl.when(exists(OFFSETS[msg]))
        def _():
            copy(msg, phase).start()

    def wait_send(msg, phase):
        @pl.when(exists(OFFSETS[msg]))
        def _():
            copy(msg, phase).wait_send()

    def comes(msg):
        return exists(tuple(-o for o in OFFSETS[msg]))

    def wait_recv(msg, phase):
        @pl.when(comes(msg))
        def _():
            copy(msg, phase).wait_recv()

    for c in (1, 2):
        e_v[c, lx] = jnp.zeros((ly, lz), f32)

    for msg in range(12):
        @pl.when(jnp.logical_not(comes(msg)))
        def _(msg=msg):
            recv[msg][...] = jnp.zeros(recv[msg].shape, f32)

    row = lax.broadcasted_iota(jnp.int32, (ly, lz), 0)
    lane = lax.broadcasted_iota(jnp.int32, (ly, lz), 1)
    row1 = lax.broadcasted_iota(jnp.int32, (ly, LANES), 0)
    lane1 = lax.broadcasted_iota(jnp.int32, (ly, LANES), 1)
    row8 = lax.broadcasted_iota(jnp.int32, (ROWS, LANES), 0)
    zero1 = jnp.zeros((ly, LANES), f32)

    def wide(t):
        return t[0] if nt == 1 else jnp.concatenate([t[k] for k in range(nt)], 1)

    def up(v, axis):
        n = v.shape[axis]
        i = lax.broadcasted_iota(jnp.int32, v.shape, axis)
        return jnp.where(i == n - 1, 0.0, pltpu.roll(v, n - 1, axis))

    def down(v, axis):
        i = lax.broadcasted_iota(jnp.int32, v.shape, axis)
        return jnp.where(i == 0, 0.0, pltpu.roll(v, 1, axis))

    def pick(tile, from_lane, to, acc):
        shift = lax.rem(to + (LANES - from_lane), LANES)
        return jnp.where(lane1 == to, pltpu.roll(tile, shift, 1), acc)

    def put_rows(dst, phase, comp, x, v, r):
        for k in range(nt):
            dst[phase, comp, k, pl.ds(x, 1), :] = v[r:r + 1, k * LANES:(k + 1) * LANES]

    def pack_top(x, phase, values):
        for i, v in enumerate(values):
            put_rows(y_t, phase, i, x, v, ly - 1)

    def pack_e(x, ex, ey, ez, phase, acc):
        put_rows(y_e, phase, 0, x, ex, 0)
        put_rows(y_e, phase, 1, x, ez, 0)
        acc = pick(ex[:, 0:LANES], 0, 2 * x, acc)
        acc = pick(ey[:, 0:LANES], 0, off + 2 * x, acc)
        return pick(ez[:, lz - LANES:lz], LANES - 1, 2 * x + 1, acc)

    def top_layers(phase):
        ex, ey, ez, hx, hz = (wide(y_t[phase, i]) for i in range(5))
        px = hx + half * (ez + (up(ey, 1) - ey))
        pz = hz - half * ((up(ey, 0) - ey) + ex)
        for i, v in enumerate((px, pz)):
            for k in range(nt):
                y_p[phase, i, k] = v[:, k * LANES:(k + 1) * LANES]
        ex, ey, ez = e_v[0, lx - 1], e_v[1, lx - 1], e_v[2, lx - 1]
        x_p[phase, 0] = h_v[1, lx - 1] - half * ((up(ex, 1) - ex) + ez)
        x_p[phase, 1] = h_v[2, lx - 1] + half * (ey + (up(ex, 0) - ex))

    def magnetic(phase):
        def one(x, acc):
            ex, ey, ez = e_v[0, x], e_v[1, x], e_v[2, x]
            dey, dez = e_v[1, x + 1] - ey, e_v[2, x + 1] - ez
            hx = h_v[0, x] - half * ((up(ez, 0) - ez) - (up(ey, 1) - ey))
            hy = h_v[1, x] - half * ((up(ex, 1) - ex) - dez)
            hz = h_v[2, x] - half * (dey - (up(ex, 0) - ex))
            h_v[0, x] = hx
            h_v[1, x] = hy
            h_v[2, x] = hz
            acc = pick(hy[:, lz - LANES:lz], LANES - 1, 2 * x + 1, acc)
            return pick(hx[:, lz - LANES:lz], LANES - 1, off + 2 * x + 1, acc)

        z_p[phase] = lax.fori_loop(0, lx, one, zero1, unroll=U_MAG)

    def save_e(phase):
        x_e[phase, 0] = e_v[1, 0]
        x_e[phase, 1] = e_v[2, 0]
        x_e[phase, 2] = e_v[0, lx - 1]

    def pre(step):
        def one(x, carry):
            hy_b, hz_b = carry
            ex, ey, ez = e_v[0, x], e_v[1, x], e_v[2, x]
            hx, hy, hz = h_v[0, x], h_v[1, x], h_v[2, x]
            if step == 0:
                mat = m_v[x]
                c = coefs[0]
                for k in range(1, nmat):
                    c = jnp.where(mat == k, coefs[k], c)
                c_v[x] = c
            else:
                c = c_v[x]
                total = None
                for comp, val in enumerate((ex, ey, ez)):
                    mid = s_v[step, comp, x].astype(f32)
                    t = val * (s_v[step - 1, comp, x].astype(f32) - mid)
                    total = t if total is None else total + t
                    diff_v[comp, x] = mid - s_v[step + 1, comp, x].astype(f32)
                fold = total[:, 0:LANES]
                for k in range(1, nt):
                    fold = fold + total[:, k * LANES:(k + 1) * LANES]
                corr_v[x] = fold
            e_v[0, x] = ex + c * ((hz - down(hz, 0)) - (hy - down(hy, 1)))
            e_v[1, x] = ey + c * ((hx - down(hx, 1)) - (hz - hz_b))
            ez = ez + c * ((hy - hy_b) - (hx - down(hx, 0)))
            for p in range(nport):
                ez = ez + src_v[step, jnp.where(port_x[p] == x, p, nport)]
            e_v[2, x] = ez
            return hy, hz

        zero = jnp.zeros((ly, lz), f32)
        lax.fori_loop(0, lx, one, (zero, zero), unroll=U_PRE)

    flags = tuple((me[a] > 0).astype(f32) for a in range(3))

    def pad_high(t):
        return jnp.concatenate([jnp.zeros((ly, lz - LANES), f32), t], 1) if lz > LANES else t

    def halos(phase):
        fx, fy, fz = flags
        d1 = pad_high(pltpu.roll(r_d1[phase], LANES - 1, 1))
        hy_x = (r_px[phase, 0] + half * x_e[phase, 1]) * fx - jnp.where(lane == lz - 1, half * d1, 0.0)
        d2 = jnp.broadcast_to(r_d2[phase, 0:1, :], (ly, lz))
        hz_x = (r_px[phase, 1] - half * x_e[phase, 0]) * fx + jnp.where(row == ly - 1, half * d2, 0.0)
        c0, c1 = c_v[0], c_v[lx - 1]
        e_v[1, 0] = e_v[1, 0] + c0 * hz_x
        e_v[2, 0] = e_v[2, 0] - c0 * hy_x
        dhy = half * r_ex[phase, 1]
        dhz = -half * r_ex[phase, 0]
        h_v[1, lx - 1] = h_v[1, lx - 1] + dhy
        h_v[2, lx - 1] = h_v[2, lx - 1] + dhz
        e_v[0, lx - 1] = e_v[0, lx - 1] + c1 * ((dhz - down(dhz, 0)) - (dhy - down(dhy, 1)))
        e_v[1, lx - 1] = e_v[1, lx - 1] - c1 * dhz
        e_v[2, lx - 1] = e_v[2, lx - 1] + c1 * dhy
        rx = lax.broadcasted_iota(jnp.int32, (lx, LANES), 0)
        cx = lax.broadcasted_iota(jnp.int32, (lx, LANES), 1)
        d4 = jnp.broadcast_to(r_d4[phase, ROWS - 1:ROWS, :], (lx, LANES))
        d4 = jnp.sum(jnp.where(cx == off + 2 * rx, d4, 0.0), axis=1, keepdims=True)
        ry = lax.broadcasted_iota(jnp.int32, (lx, lz), 0)
        cy = lax.broadcasted_iota(jnp.int32, (lx, lz), 1)
        hx_y = (wide(r_py[phase, 0]) - half * wide(y_e[phase, 1])) * fy + jnp.where(cy == lz - 1, half * d4, 0.0)
        d3 = jnp.broadcast_to(r_d3[phase, ROWS - 1:ROWS, :], (lx, lz))
        hz_y = (wide(r_py[phase, 1]) + half * wide(y_e[phase, 0])) * fy - jnp.where(ry == lx - 1, half * d3, 0.0)
        dhx = -half * wide(r_ey[phase, 1])
        dhz = half * wide(r_ey[phase, 0])
        values = (-hz_y, hx_y, dhz, (dhx - down(dhx, 1)) - (dhz - down(dhz, 0)), -dhx)
        for i, v in enumerate(values):
            for k in range(nt):
                rows_v[i, k] = v[:, k * LANES:(k + 1) * LANES]
        own = pltpu.roll(z_e[phase], 1, 1)
        low = lane1 < off
        zh = (r_pz[phase] + jnp.where(low, -half * own, half * own)) * fz
        d5 = jnp.broadcast_to(pltpu.roll(r_d5[phase], off, 1)[0:1, :], (ly, LANES))
        zh = zh - jnp.where((row1 == ly - 1) & (lane1 >= off), half * d5, 0.0)
        d6 = pltpu.roll(r_d6[phase], off, 1)
        zh = zh + jnp.where(lane1 == off - 1, half * d6, 0.0)
        ze = half * r_ez[phase]
        odd = lax.rem(lane1, 2) == 1
        cols = jnp.where(odd, jnp.where(low, zh, -zh), ze)
        dhy = jnp.where(odd | (lane1 >= off), 0.0, -ze)
        dhx = jnp.where(odd | (lane1 >= off), 0.0, pltpu.roll(ze, LANES - off, 1))
        shift_x = jnp.where(lane1 < 2, 0.0, pltpu.roll(dhy, 2, 1))
        last = (dhy - shift_x) - (dhx - down(dhx, 0))
        return cols, last

    top, bottom = row8 == 0, row8 == ROWS - 1
    lane8 = lax.broadcasted_iota(jnp.int32, (ROWS, LANES), 1)
    first_lane, last_lane = lane8 == 0, lane8 == LANES - 1
    nr = ly // ROWS

    def post(step, cols, last):
        def one(x, acc):
            low_col = pltpu.roll(cols, lax.rem(2 * LANES - (2 * x + 1), LANES), 1)
            high_col = pltpu.roll(cols, lax.rem(2 * LANES - (off + 2 * x + 1), LANES), 1)
            last_col = pltpu.roll(last, lax.rem(2 * LANES - (2 * x + 1), LANES), 1)
            def delta(r, k, col0, col1, row0, row1_):
                terms = []
                cut = slice(r * ROWS, (r + 1) * ROWS)
                if col0 is not None and k == 0:
                    terms.append(jnp.where(first_lane, col0[cut], 0.0))
                if col1 is not None and k == nt - 1:
                    terms.append(jnp.where(last_lane, col1[cut], 0.0))
                if row0 is not None and r == 0:
                    t = jnp.broadcast_to(rows_v[row0, k, pl.ds(x, 1), :], (ROWS, LANES))
                    terms.append(jnp.where(top, t, 0.0))
                if row1_ is not None and r == nr - 1:
                    t = jnp.broadcast_to(rows_v[row1_, k, pl.ds(x, 1), :], (ROWS, LANES))
                    terms.append(jnp.where(bottom, t, 0.0))
                return sum(terms[1:], terms[0]) if terms else None

            new = []
            for comp, args in enumerate(((low_col, low_col, 0, 2), (high_col, high_col, None, 3), (None, last_col, 1, 4))):
                strips = []
                for k in range(nt):
                    strip = []
                    for r in range(nr):
                        at_ = (comp, x, pl.ds(r * ROWS, ROWS), pl.ds(k * LANES, LANES))
                        d = delta(r, k, *args)
                        v = e_v[at_]
                        if d is not None:
                            v = v + c_v[x, r * ROWS:(r + 1) * ROWS, k * LANES:(k + 1) * LANES] * d
                            e_v[at_] = v
                        strip.append(v)
                    strips.append(jnp.concatenate(strip, 0) if nr > 1 else strip[0])
                new.append(strips)
            for comp, args in enumerate((
                ((None, high_col, None, None, 1), (None, None, None, 4, -1)),
                ((None, low_col, None, None, -1),),
                ((None, None, None, 2, 1),),
            )):
                for r in range(nr):
                    for k in range(nt):
                        at_ = (comp, x, pl.ds(r * ROWS, ROWS), pl.ds(k * LANES, LANES))
                        v = h_v[at_] if step + 1 < STEPS and r == nr - 1 and comp != 1 else None
                        for *which, sign in args:
                            d = delta(r, k, *which)
                            if d is not None:
                                v = h_v[at_] if v is None else v
                                v = v + d if sign > 0 else v - d
                        if v is not None:
                            h_v[at_] = v
                        if step + 1 < STEPS and r == nr - 1 and comp != 1:
                            y_t[step + 1, 3 + comp // 2, k, pl.ds(x, 1), :] = v[ROWS - 1:ROWS]
            if step + 1 < STEPS:
                values = [wide(n) for n in new]
                pack_top(x, step + 1, values)
                return pack_e(x, *values, step + 1, acc)
            fold = corr_v[x]
            for comp in range(3):
                for k in range(nt):
                    fold = fold + new[comp][k] * diff_v[comp, x, :, k * LANES:(k + 1) * LANES]
            return jnp.where(lane1 == x, jnp.sum(fold, axis=1, keepdims=True), acc)

        return lax.fori_loop(0, lx, one, zero1, unroll=U_POST)

    pl.semaphore_wait(barrier, count)
    for msg in (D2, D3, D1, D6, EX):
        send(msg, 0)

    def first_pack(x, acc):
        ex, ey, ez = e_v[0, x], e_v[1, x], e_v[2, x]
        pack_top(x, 0, (ex, ey, ez))
        return pack_e(x, ex, ey, ez, 0, acc)

    def first_top(x, carry):
        put_rows(y_t, 0, 3, x, h_v[0, x], ly - 1)
        put_rows(y_t, 0, 4, x, h_v[2, x], ly - 1)
        return carry

    acc = zero1
    for k in range(CHUNKS):
        load_e[k].wait()
        acc = lax.fori_loop(k * step_x, (k + 1) * step_x, first_pack, acc, unroll=True)
    z_e[0] = acc
    for msg in (EY, D4, D5, EZ):
        send(msg, 0)
    for k in range(CHUNKS):
        load_h[k].wait()
        lax.fori_loop(k * step_x, (k + 1) * step_x, first_top, 0, unroll=True)
    top_layers(0)
    send(PY, 0)
    send(PX, 0)
    magnetic(0)
    send(PZ, 0)
    save_e(0)

    plane = extent[1] * extent[2]
    port_x = []
    for p in range(nport):
        cell = ports[p]
        px = lax.div(cell, plane)
        rest = lax.rem(cell, plane)
        py = lax.div(rest, extent[2]) - start[1]
        pz = lax.rem(rest, extent[2]) - start[2]
        port_x.append(px - start[0])
        hit = (row == py) & (lane == pz)
        for s in range(STEPS):
            src_v[s, p] = jnp.where(hit, amps[s, p], 0.0)
    for s in range(STEPS):
        src_v[s, nport] = jnp.zeros((ly, lz), f32)
    coefs = [half / jnp.full((ly, lz), perm[k], f32) for k in range(nmat)]
    load_m.wait()
    pre(0)
    for msg in range(12):
        wait_recv(msg, 0)
    cols, last = halos(0)
    z_e[1] = post(0, cols, last)
    save_e(1)
    for msg in (D2, D3, D1, D6, D4, D5, EY, EX):
        send(msg, 1)
    top_layers(1)
    for msg in (PY, PX, EZ):
        send(msg, 1)
    magnetic(1)
    send(PZ, 1)
    load_s.wait()
    pre(1)
    for msg in range(12):
        wait_recv(msg, 1)
    cols, last = halos(1)
    acc = post(1, cols, last)

    own_rows = ly // nz_dev
    tile = g_out.shape[0]
    g_v[...] = acc
    g_v[:, 0:lx] = acc[:, 0:lx] * mask[...].astype(f32)

    def tile_of(k):
        return pl.ds(pl.multiple_of((k * own_rows) // tile * tile, ROWS), tile)

    gcopies = []
    for d in range(1, nz_dev):
        peer = lax.rem(me[2] + d, nz_dev)
        gcopies.append(pltpu.make_async_remote_copy(
            src_ref=g_v.at[tile_of(peer)], dst_ref=r_g.at[d - 1],
            send_sem=gs_sem.at[d - 1], recv_sem=gr_sem.at[d - 1],
            device_id=(me[0], me[1], peer), device_id_type=pl.DeviceIdType.MESH))
    for c in gcopies:
        c.start()
    for phase in range(STEPS):
        for msg in range(12):
            wait_send(msg, phase)
    total = g_v[tile_of(me[2])]
    for d, c in enumerate(gcopies):
        c.wait_recv()
        total = total + r_g[d]
    shift = lax.rem(tile - lax.rem(me[2] * own_rows, tile), tile)
    g_out[...] = pltpu.roll(total, shift, 0)
    for c in gcopies:
        c.wait_send()


def write_out(e_v, h_v, g_v, e_out, h_out, g_out, sem):
    lx = h_v.shape[1]
    outs = [
        pltpu.make_async_copy(e_v.at[:, 0:lx], e_out, sem.at[0]),
        pltpu.make_async_copy(h_v, h_out, sem.at[1]),
    ]
    for c in outs:
        c.start()
    g_out[...] = g_v[0:g_out.shape[0], 0:g_out.shape[1]]
    for c in outs:
        c.wait()


def solution(mesh):
    mesh_sizes = tuple(mesh.shape[a] for a in AXES)

    def body(e_adjoint, h_adjoint, snapshots, material, permittivity, design_mask, ports, amplitudes):
        _, lx, ly, lz = e_adjoint.shape
        extent = (lx * mesh_sizes[0], ly * mesh_sizes[1], lz * mesh_sizes[2])
        nport = ports.shape[0]
        nt = lz // LANES
        f32 = jnp.float32
        own = ly // mesh_sizes[2]
        tile = max(ROWS, own)
        any_spec = pl.BlockSpec(memory_space=pl.ANY)
        smem = pl.BlockSpec(memory_space=pltpu.SMEM)
        vmem = pl.BlockSpec(memory_space=pltpu.VMEM)
        e, h, g = pl.pallas_call(
            lambda *refs: kernel(mesh_sizes, extent, *refs),
            out_shape=(
                pltpu.VMEM((3, lx + 1, ly, lz), f32),
                pltpu.VMEM((3, lx, ly, lz), f32),
                pltpu.VMEM((tile, LANES), f32),
            ),
            in_specs=[smem, smem, smem, vmem, any_spec, any_spec, any_spec, any_spec],
            out_specs=(vmem, vmem, vmem),
            scratch_shapes=[
                pltpu.VMEM(snapshots.shape, snapshots.dtype),
                pltpu.VMEM((lx, ly, lz), jnp.int32),
                pltpu.VMEM((lx, ly, lz), f32),
                pltpu.VMEM((lx, ly, LANES), f32),
                pltpu.VMEM((3, lx, ly, lz), f32),
                pltpu.VMEM((STEPS, nport + 1, ly, lz), f32),
                pltpu.VMEM((STEPS, 3, ly, lz), f32),
                pltpu.VMEM((STEPS, 2, nt, lx, LANES), f32),
                pltpu.VMEM((STEPS, ly, LANES), f32),
                pltpu.VMEM((STEPS, 2, ly, lz), f32),
                pltpu.VMEM((STEPS, 2, nt, lx, LANES), f32),
                pltpu.VMEM((STEPS, ly, LANES), f32),
                pltpu.VMEM((STEPS, 5, nt, lx, LANES), f32),
                pltpu.VMEM((5, nt, lx, LANES), f32),
                pltpu.VMEM((ly, LANES), f32),
                pltpu.VMEM((STEPS, 2, ly, lz), f32),
                pltpu.VMEM((STEPS, 2, nt, lx, LANES), f32),
                pltpu.VMEM((STEPS, ly, LANES), f32),
                pltpu.VMEM((STEPS, 2, ly, lz), f32),
                pltpu.VMEM((STEPS, 2, nt, lx, LANES), f32),
                pltpu.VMEM((STEPS, ly, LANES), f32),
                pltpu.VMEM((STEPS, ly, LANES), f32),
                pltpu.VMEM((STEPS, ROWS, lz), f32),
                pltpu.VMEM((STEPS, ROWS, lz), f32),
                pltpu.VMEM((STEPS, ROWS, LANES), f32),
                pltpu.VMEM((STEPS, ROWS, LANES), f32),
                pltpu.VMEM((STEPS, ly, LANES), f32),
                pltpu.VMEM((3, tile, LANES), f32),
                pltpu.SemaphoreType.DMA((2 + 2 * CHUNKS,)),
                pltpu.SemaphoreType.DMA((STEPS, 12)),
                pltpu.SemaphoreType.DMA((STEPS, 12)),
                pltpu.SemaphoreType.DMA((3,)),
                pltpu.SemaphoreType.DMA((3,)),
            ],
            compiler_params=pltpu.CompilerParams(collective_id=0, has_side_effects=True),
            name="reverse_steps",
        )(permittivity, ports, amplitudes, design_mask.T, e_adjoint, h_adjoint, snapshots, material)
        e, h, g = (pltpu.with_memory_space_constraint(v, pltpu.VMEM) for v in (e, h, g))
        e, h, g = pl.pallas_call(
            write_out,
            out_shape=(
                jax.ShapeDtypeStruct(e_adjoint.shape, f32),
                jax.ShapeDtypeStruct(h_adjoint.shape, f32),
                jax.ShapeDtypeStruct((own, lx), f32),
            ),
            in_specs=[vmem, vmem, vmem],
            out_specs=(any_spec, any_spec, vmem),
            scratch_shapes=[pltpu.SemaphoreType.DMA((2,))],
            name="write_out",
        )(e, h, g)
        return e, h, g.T

    placed = (
        P(None, "gx", "gy", "gz"),
        P(None, "gx", "gy", "gz"),
        P(None, None, "gx", "gy", "gz"),
        P("gx", "gy", "gz"),
        P(),
        P("gx", "gy"),
        P(),
        P(),
    )
    return jax.shard_map(
        body,
        mesh=mesh,
        in_specs=placed,
        out_specs=(P(None, "gx", "gy", "gz"), P(None, "gx", "gy", "gz"), P("gx", ("gy", "gz"))),
        check_vma=False,
    )
```

time: 28.3 us -> 26.3 us (0.929)
  the two profiles are of different devices: /device:TPU:160 before, /device:TPU:33 now
where the time goes in v4:
time: 26.3 us; the launch traced here: 26.1 us
  Pallas kernels  25.5 us (97%)
  between operations  0.64 us (2%)
    pallas_call x1, Pallas kernels, body(): pl.pallas_call(lambda *refs: kernel(mesh_sizes, extent, *refs), out_shape...  23.2 us
    pallas_call x1, Pallas kernels, body(): pl.pallas_call(write_out, out_shape=(jax.ShapeDtypeStruct(e_adjoint.shape...  2.26 us

profile of v4, /device:TPU:33, one launch (start us, length us, event | category | flops | bytes accessed | tf_op | source)
XLA Modules:
  0.0 26.1 jit_solution(10656962160034597902)
XLA Ops:
  0.6 23.2 %reverse_steps.1 = (f32[3,33,16,256]{3,2,1,0:T(8,128)S(1)}, f32[3,32,16,256]{3,2,1,0:T(8,128)S(1)}, f32[8,128]{1,0:T(8,128)S(1)}) custom-call(f32[8]{0:T(128)} %refs_0_.1, s32[3]{0:T(128)} %refs_1_.1, f32[2,3]{1,0:T(2,128)} %refs_2_.1, s32[16,32]{1,0:T(8,128)} %bitcast.2, f32[3,32,16,256]{3,2,1,0:T(8,128)} %refs_4_.1, f32[3,32,16,256]{3,2,1,0:T(8,128)} %refs_5_.1, ...), custom_call_target="tpu_custom_call" | custom-call | tf_op jit(solution)/shard_map/reverse_steps/pallas_call | solution.py:486
  23.9 2.3 %write_out.1 = (f32[3,32,16,256]{3,2,1,0:T(8,128)}, f32[3,32,16,256]{3,2,1,0:T(8,128)}, f32[4,32]{1,0:T(4,128)}) custom-call(f32[3,33,16,256]{3,2,1,0:T(8,128)S(1)} %get-tuple-element.9.e_v, f32[3,32,16,256]{3,2,1,0:T(8,128)S(1)} %get-tuple-element.10.h_v, f32[8,128]{1,0:T(8,128)S(1)} %get-tuple-element.11.g_v), custom_call_target="tpu_custom_call" | custom-call | tf_op jit(solution)/shard_map/write_out/pallas_call | solution.py:534

commit v5 on v4

--- a/solution.py
+++ b/solution.py
@@ -10,8 +10,7 @@
 LANES = 128
 ROWS = 8
 half = 0.5
-U_MAG, U_PRE, U_POST = 8, 8, 8
-CHUNKS = 4
+U_MAG, U_PRE, U_POST, U_PACK = 8, 8, 8, 8
 
 EX, EY, EZ, PX, PY, PZ, D1, D2, D3, D4, D5, D6 = range(12)
 OFFSETS = (
@@ -21,18 +20,18 @@
 )
 
 
-def kernel(mesh_sizes, extent, perm, ports, amps, mask, e_in, h_in, s_in, m_in,
+def kernel(mesh_sizes, extent, perm_in, ports_in, amps_in, mask_in, e_in, h_in, s_in, m_in,
            e_v, h_v, g_out,
-           s_v, m_v, c_v, corr_v, diff_v, src_v,
-           x_e, y_e, z_e, x_p, y_p, z_p, y_t, rows_v, g_v,
+           s_v, m_v, c_v, src_v,
+           x_e, y_e, z_e, x_p, y_p, z_p, y_t, y_b, rows_v, g_v,
            r_ex, r_ey, r_ez, r_px, r_py, r_pz, r_d1, r_d2, r_d3, r_d4, r_d5, r_d6, r_g,
-           in_sem, send_sem, recv_sem, gs_sem, gr_sem):
+           perm, ports, amps, mask_v, in_sem, send_sem, recv_sem, gs_sem, gr_sem):
     _, lx, ly, lz = e_in.shape
     nt = lz // LANES
     off = 2 * lx
     f32 = jnp.float32
-    nmat = perm.shape[0]
-    nport = ports.shape[0]
+    nmat = perm_in.shape[0]
+    nport = ports_in.shape[0]
     me = tuple(lax.axis_index(a) for a in AXES)
     start = (me[0] * lx, me[1] * ly, me[2] * lz)
     nz_dev = mesh_sizes[2]
@@ -50,15 +49,18 @@
     def at(o):
         return tuple(me[a] + o[a] for a in range(3))
 
-    step_x = lx // CHUNKS
+    high, low_part = pl.ds(ly - ROWS, ROWS), pl.ds(0, ly - ROWS)
     load_e, load_h = [], []
-    for k in range(CHUNKS):
-        d = pl.ds(k * step_x, step_x)
-        load_e.append(pltpu.make_async_copy(e_in.at[:, d], e_v.at[:, d], in_sem.at[2 + k]))
-        load_h.append(pltpu.make_async_copy(h_in.at[:, d], h_v.at[:, d], in_sem.at[2 + CHUNKS + k]))
+    for k, d in enumerate((high, low_part)):
+        load_e.append(pltpu.make_async_copy(e_in.at[:, :, d], e_v.at[:, 0:lx, d], in_sem.at[2 + 2 * k]))
+        load_h.append(pltpu.make_async_copy(h_in.at[:, :, d], h_v.at[:, :, d], in_sem.at[3 + 2 * k]))
     load_m = pltpu.make_async_copy(m_in, m_v, in_sem.at[0])
     load_s = pltpu.make_async_copy(s_in, s_v, in_sem.at[1])
-    for c in load_e + load_h + [load_m, load_s]:
+    load_small = [
+        pltpu.make_async_copy(a, b, in_sem.at[6 + i])
+        for i, (a, b) in enumerate(((perm_in, perm), (ports_in, ports), (amps_in, amps), (mask_in, mask_v)))
+    ]
+    for c in [load_e[0], load_h[0], load_e[1], load_h[1]] + load_small + [load_m, load_s]:
         c.start()
 
     barrier = pltpu.get_barrier_semaphore()
@@ -157,28 +159,24 @@
         shift = lax.rem(to + (LANES - from_lane), LANES)
         return jnp.where(lane1 == to, pltpu.roll(tile, shift, 1), acc)
 
-    def put_rows(dst, phase, comp, x, v, r):
+    def put(dst, i, x, v, r):
         for k in range(nt):
-            dst[phase, comp, k, pl.ds(x, 1), :] = v[r:r + 1, k * LANES:(k + 1) * LANES]
-
-    def pack_top(x, phase, values):
-        for i, v in enumerate(values):
-            put_rows(y_t, phase, i, x, v, ly - 1)
-
-    def pack_e(x, ex, ey, ez, phase, acc):
-        put_rows(y_e, phase, 0, x, ex, 0)
-        put_rows(y_e, phase, 1, x, ez, 0)
+            dst[i, k, pl.ds(x, 1), :] = v[r:r + 1, k * LANES:(k + 1) * LANES]
+
+    def put_wide(dst, i, v):
+        for k in range(nt):
+            dst[i, k] = v[:, k * LANES:(k + 1) * LANES]
+
+    def pick_e(x, ex, ey, ez, acc):
         acc = pick(ex[:, 0:LANES], 0, 2 * x, acc)
         acc = pick(ey[:, 0:LANES], 0, off + 2 * x, acc)
         return pick(ez[:, lz - LANES:lz], LANES - 1, 2 * x + 1, acc)
 
-    def top_layers(phase):
-        ex, ey, ez, hx, hz = (wide(y_t[phase, i]) for i in range(5))
-        px = hx + half * (ez + (up(ey, 1) - ey))
-        pz = hz - half * ((up(ey, 0) - ey) + ex)
-        for i, v in enumerate((px, pz)):
-            for k in range(nt):
-                y_p[phase, i, k] = v[:, k * LANES:(k + 1) * LANES]
+    def top_y(phase, ex, ey, ez, hx, hz):
+        put_wide(y_p.at[phase], 0, hx + half * (ez + (up(ey, 1) - ey)))
+        put_wide(y_p.at[phase], 1, hz - half * ((up(ey, 0) - ey) + ex))
+
+    def top_x(phase):
         ex, ey, ez = e_v[0, lx - 1], e_v[1, lx - 1], e_v[2, lx - 1]
         x_p[phase, 0] = h_v[1, lx - 1] - half * ((up(ex, 1) - ex) + ez)
         x_p[phase, 1] = h_v[2, lx - 1] + half * (ey + (up(ex, 0) - ex))
@@ -205,7 +203,7 @@
 
     def pre(step):
         def one(x, carry):
-            hy_b, hz_b = carry
+            hy_b, hz_b, acc_c, acc_l, acc_g = carry
             ex, ey, ez = e_v[0, x], e_v[1, x], e_v[2, x]
             hx, hy, hz = h_v[0, x], h_v[1, x], h_v[2, x]
             if step == 0:
@@ -216,26 +214,42 @@
                 c_v[x] = c
             else:
                 c = c_v[x]
-                total = None
+                total, change = None, []
                 for comp, val in enumerate((ex, ey, ez)):
                     mid = s_v[step, comp, x].astype(f32)
                     t = val * (s_v[step - 1, comp, x].astype(f32) - mid)
                     total = t if total is None else total + t
-                    diff_v[comp, x] = mid - s_v[step + 1, comp, x].astype(f32)
+                    change.append(mid - s_v[step + 1, comp, x].astype(f32))
+            ex = ex + c * ((hz - down(hz, 0)) - (hy - down(hy, 1)))
+            ey = ey + c * ((hx - down(hx, 1)) - (hz - hz_b))
+            ez = ez + c * ((hy - hy_b) - (hx - down(hx, 0)))
+            for p in range(nport):
+                ez = ez + src_v[step, jnp.where(port_x[p] == x, p, nport)]
+            e_v[0, x] = ex
+            e_v[1, x] = ey
+            e_v[2, x] = ez
+            if step == 0:
+                for i, (v, r) in enumerate(((ex, 0), (ez, 0), (ex, -1), (ey, -1), (ez, -1), (hx, -1), (hz, -1), (c, 0), (c, -1))):
+                    put(y_b, i, x, v, r % ly)
+            else:
+                for val, d in zip((ex, ey, ez), change):
+                    total = total + val * d
                 fold = total[:, 0:LANES]
                 for k in range(1, nt):
                     fold = fold + total[:, k * LANES:(k + 1) * LANES]
-                corr_v[x] = fold
-            e_v[0, x] = ex + c * ((hz - down(hz, 0)) - (hy - down(hy, 1)))
-            e_v[1, x] = ey + c * ((hx - down(hx, 1)) - (hz - hz_b))
-            ez = ez + c * ((hy - hy_b) - (hx - down(hx, 0)))
-            for p in range(nport):
-                ez = ez + src_v[step, jnp.where(port_x[p] == x, p, nport)]
-            e_v[2, x] = ez
-            return hy, hz
+                acc_g = jnp.where(lane1 == 2 * x, jnp.sum(fold, axis=1, keepdims=True), acc_g)
+                wx, wy, wz = (c * d for d in change)
+                for i, (v, r) in enumerate(((wx, 0), (wz, 0), (wx, -1), (wy, -1), (wz, -1))):
+                    put(y_b, i, x, v, r % ly)
+                acc_c = pick(wx[:, 0:LANES], 0, 2 * x + 1, acc_c)
+                acc_c = pick(wy[:, 0:LANES], 0, off + 2 * x + 1, acc_c)
+                acc_c = pick(wx[:, lz - LANES:lz], LANES - 1, 2 * x, acc_c)
+                acc_c = pick(wy[:, lz - LANES:lz], LANES - 1, off + 2 * x, acc_c)
+                acc_l = pick(wz[:, lz - LANES:lz], LANES - 1, 2 * x, acc_l)
+            return hy, hz, acc_c, acc_l, acc_g
 
         zero = jnp.zeros((ly, lz), f32)
-        lax.fori_loop(0, lx, one, (zero, zero), unroll=U_PRE)
+        return lax.fori_loop(0, lx, one, (zero, zero, zero1, zero1, zero1), unroll=U_PRE)[2:]
 
     flags = tuple((me[a] > 0).astype(f32) for a in range(3))
 
@@ -249,15 +263,17 @@
         d2 = jnp.broadcast_to(r_d2[phase, 0:1, :], (ly, lz))
         hz_x = (r_px[phase, 1] - half * x_e[phase, 0]) * fx + jnp.where(row == ly - 1, half * d2, 0.0)
         c0, c1 = c_v[0], c_v[lx - 1]
-        e_v[1, 0] = e_v[1, 0] + c0 * hz_x
-        e_v[2, 0] = e_v[2, 0] - c0 * hy_x
         dhy = half * r_ex[phase, 1]
         dhz = -half * r_ex[phase, 0]
         h_v[1, lx - 1] = h_v[1, lx - 1] + dhy
         h_v[2, lx - 1] = h_v[2, lx - 1] + dhz
-        e_v[0, lx - 1] = e_v[0, lx - 1] + c1 * ((dhz - down(dhz, 0)) - (dhy - down(dhy, 1)))
-        e_v[1, lx - 1] = e_v[1, lx - 1] - c1 * dhz
-        e_v[2, lx - 1] = e_v[2, lx - 1] + c1 * dhy
+        planes = (
+            (1, 0, c0 * hz_x), (2, 0, -c0 * hy_x),
+            (0, lx - 1, c1 * ((dhz - down(dhz, 0)) - (dhy - down(dhy, 1)))),
+            (1, lx - 1, -c1 * dhz), (2, lx - 1, c1 * dhy),
+        )
+        for comp, x, d in planes:
+            e_v[comp, x] = e_v[comp, x] + d
         rx = lax.broadcasted_iota(jnp.int32, (lx, LANES), 0)
         cx = lax.broadcasted_iota(jnp.int32, (lx, LANES), 1)
         d4 = jnp.broadcast_to(r_d4[phase, ROWS - 1:ROWS, :], (lx, LANES))
@@ -271,8 +287,7 @@
         dhz = half * wide(r_ey[phase, 0])
         values = (-hz_y, hx_y, dhz, (dhx - down(dhx, 1)) - (dhz - down(dhz, 0)), -dhx)
         for i, v in enumerate(values):
-            for k in range(nt):
-                rows_v[i, k] = v[:, k * LANES:(k + 1) * LANES]
+            put_wide(rows_v, i, v)
         own = pltpu.roll(z_e[phase], 1, 1)
         low = lane1 < off
         zh = (r_pz[phase] + jnp.where(low, -half * own, half * own)) * fz
@@ -287,7 +302,51 @@
         dhx = jnp.where(odd | (lane1 >= off), 0.0, pltpu.roll(ze, LANES - off, 1))
         shift_x = jnp.where(lane1 < 2, 0.0, pltpu.roll(dhy, 2, 1))
         last = (dhy - shift_x) - (dhx - down(dhx, 0))
-        return cols, last
+        return planes, values, cols, last
+
+    rx1 = lax.broadcasted_iota(jnp.int32, (lx, LANES), 0)
+    cx1 = lax.broadcasted_iota(jnp.int32, (lx, LANES), 1)
+    cyw = lax.broadcasted_iota(jnp.int32, (lx, lz), 1)
+
+    def first_rows(values, cols, last):
+        for x in (0, lx - 1):
+            for i, (src, comp, r) in enumerate((
+                (e_v, 0, 0), (e_v, 2, 0), (e_v, 0, -1), (e_v, 1, -1), (e_v, 2, -1), (h_v, 0, -1), (h_v, 2, -1))):
+                put(y_b, i, x, src[comp, x], r % ly)
+
+        def edge(col, y, at_lane, to):
+            t = jnp.where(cx1 == 2 * rx1 + at_lane, jnp.broadcast_to(col[y:y + 1], (lx, LANES)), 0.0)
+            return jnp.where(cyw == to, jnp.sum(t, axis=1, keepdims=True), 0.0)
+
+        b = [wide(y_b[i]) for i in range(9)]
+        y, end = ly - 1, lz - 1
+        hx_edge = edge(cols, y, off, end)
+        put_wide(y_e.at[1], 0, b[0] + b[7] * (values[0] + edge(cols, 0, 1, 0) + edge(cols, 0, 0, end)))
+        put_wide(y_e.at[1], 1, b[1] + b[7] * (values[1] + edge(last, 0, 0, end)))
+        ex = b[2] + b[8] * (values[2] + edge(cols, y, 1, 0) + edge(cols, y, 0, end))
+        ey = b[3] + b[8] * (values[3] + edge(cols, y, off + 1, 0) + hx_edge)
+        ez = b[4] + b[8] * (values[4] + edge(last, y, 0, end))
+        top_y(1, ex, ey, ez, b[5] - values[4] + hx_edge, b[6] + values[2])
+
+    def gradient_part(planes, values, cols, last, acc_c, acc_l, acc_g):
+        w = [wide(y_b[i]) for i in range(5)]
+        total = acc_g
+        for y, t in ((0, values[0] * w[0] + values[1] * w[1]), (ly - 1, values[2] * w[2] + values[3] * w[3] + values[4] * w[4])):
+            t = jnp.sum(t, axis=1, keepdims=True)
+            t = jnp.sum(jnp.where(cx1 == 2 * rx1, t, 0.0), axis=0, keepdims=True)
+            total = total + jnp.where(row1 == y, t, 0.0)
+        p = cols * acc_c
+        q = p + pltpu.roll(p, LANES - 1, 1)
+        q = q + pltpu.roll(q, LANES - off, 1) + last * acc_l
+        total = total + jnp.where((lane1 < off) & (lax.rem(lane1, 2) == 0), q, 0.0)
+        for x in (0, lx - 1):
+            t = None
+            for comp, at_x, d in planes:
+                if at_x == x:
+                    change = s_v[STEPS - 1, comp, x].astype(f32) - s_v[STEPS, comp, x].astype(f32)
+                    t = d * change if t is None else t + d * change
+            total = total + jnp.where(lane1 == 2 * x, jnp.sum(t, axis=1, keepdims=True), 0.0)
+        return total
 
     top, bottom = row8 == 0, row8 == ROWS - 1
     lane8 = lax.broadcasted_iota(jnp.int32, (ROWS, LANES), 1)
@@ -337,7 +396,7 @@
                 for r in range(nr):
                     for k in range(nt):
                         at_ = (comp, x, pl.ds(r * ROWS, ROWS), pl.ds(k * LANES, LANES))
-                        v = h_v[at_] if step + 1 < STEPS and r == nr - 1 and comp != 1 else None
+                        v = None
                         for *which, sign in args:
                             d = delta(r, k, *which)
                             if d is not None:
@@ -345,17 +404,7 @@
                                 v = v + d if sign > 0 else v - d
                         if v is not None:
                             h_v[at_] = v
-                        if step + 1 < STEPS and r == nr - 1 and comp != 1:
-                            y_t[step + 1, 3 + comp // 2, k, pl.ds(x, 1), :] = v[ROWS - 1:ROWS]
-            if step + 1 < STEPS:
-                values = [wide(n) for n in new]
-                pack_top(x, step + 1, values)
-                return pack_e(x, *values, step + 1, acc)
-            fold = corr_v[x]
-            for comp in range(3):
-                for k in range(nt):
-                    fold = fold + new[comp][k] * diff_v[comp, x, :, k * LANES:(k + 1) * LANES]
-            return jnp.where(lane1 == x, jnp.sum(fold, axis=1, keepdims=True), acc)
+            return pick_e(x, *(wide(n) for n in new), acc) if step + 1 < STEPS else acc
 
         return lax.fori_loop(0, lx, one, zero1, unroll=U_POST)
 
@@ -363,33 +412,35 @@
     for msg in (D2, D3, D1, D6, EX):
         send(msg, 0)
 
+    def first_top(x, carry):
+        for i, (src, comp) in enumerate(((e_v, 0), (e_v, 1), (e_v, 2), (h_v, 0), (h_v, 2))):
+            put(y_t, i, x, src[comp, x, ly - ROWS:ly, :], ROWS - 1)
+        return carry
+
     def first_pack(x, acc):
         ex, ey, ez = e_v[0, x], e_v[1, x], e_v[2, x]
-        pack_top(x, 0, (ex, ey, ez))
-        return pack_e(x, ex, ey, ez, 0, acc)
-
-    def first_top(x, carry):
-        put_rows(y_t, 0, 3, x, h_v[0, x], ly - 1)
-        put_rows(y_t, 0, 4, x, h_v[2, x], ly - 1)
-        return carry
-
-    acc = zero1
-    for k in range(CHUNKS):
-        load_e[k].wait()
-        acc = lax.fori_loop(k * step_x, (k + 1) * step_x, first_pack, acc, unroll=True)
-    z_e[0] = acc
+        put(y_e.at[0], 0, x, ex, 0)
+        put(y_e.at[0], 1, x, ez, 0)
+        return pick_e(x, ex, ey, ez, acc)
+
+    load_e[0].wait()
+    load_h[0].wait()
+    lax.fori_loop(0, lx, first_top, 0, unroll=U_PACK)
+    top_y(0, *(wide(y_t[i]) for i in range(5)))
+    send(PY, 0)
+    load_e[1].wait()
+    z_e[0] = lax.fori_loop(0, lx, first_pack, zero1, unroll=U_PACK)
     for msg in (EY, D4, D5, EZ):
         send(msg, 0)
-    for k in range(CHUNKS):
-        load_h[k].wait()
-        lax.fori_loop(k * step_x, (k + 1) * step_x, first_top, 0, unroll=True)
-    top_layers(0)
-    send(PY, 0)
+    load_h[1].wait()
+    top_x(0)
     send(PX, 0)
     magnetic(0)
     send(PZ, 0)
     save_e(0)
 
+    for c in load_small:
+        c.wait()
     plane = extent[1] * extent[2]
     port_x = []
     for p in range(nport):
@@ -409,27 +460,31 @@
     pre(0)
     for msg in range(12):
         wait_recv(msg, 0)
-    cols, last = halos(0)
+    planes, values, cols, last = halos(0)
+    first_rows(values, cols, last)
+    for msg in (EY, PY):
+        send(msg, 1)
     z_e[1] = post(0, cols, last)
     save_e(1)
-    for msg in (D2, D3, D1, D6, D4, D5, EY, EX):
+    for msg in (D2, D3, D1, D6, D4, D5, EX):
         send(msg, 1)
-    top_layers(1)
-    for msg in (PY, PX, EZ):
+    top_x(1)
+    for msg in (PX, EZ):
         send(msg, 1)
     magnetic(1)
     send(PZ, 1)
     load_s.wait()
-    pre(1)
+    weights = pre(1)
+    spread = lax.broadcasted_iota(jnp.int32, (lx, LANES), 1) == 2 * lax.broadcasted_iota(jnp.int32, (lx, LANES), 0)
+    mask = jnp.dot(mask_v[...].astype(f32), spread.astype(f32), preferred_element_type=f32)
     for msg in range(12):
         wait_recv(msg, 1)
-    cols, last = halos(1)
-    acc = post(1, cols, last)
+    planes, values, cols, last = halos(1)
+    acc = gradient_part(planes, values, cols, last, *weights)
 
     own_rows = ly // nz_dev
     tile = g_out.shape[0]
-    g_v[...] = acc
-    g_v[:, 0:lx] = acc[:, 0:lx] * mask[...].astype(f32)
+    g_v[...] = acc * mask
 
     def tile_of(k):
         return pl.ds(pl.multiple_of((k * own_rows) // tile * tile, ROWS), tile)
@@ -443,6 +498,7 @@
             device_id=(me[0], me[1], peer), device_id_type=pl.DeviceIdType.MESH))
     for c in gcopies:
         c.start()
+    post(1, cols, last)
     for phase in range(STEPS):
         for msg in range(12):
             wait_send(msg, phase)
@@ -464,7 +520,10 @@
     ]
     for c in outs:
         c.start()
-    g_out[...] = g_v[0:g_out.shape[0], 0:g_out.shape[1]]
+    own, _ = g_out.shape
+    pick = lax.broadcasted_iota(jnp.int32, (LANES, LANES), 0) == 2 * lax.broadcasted_iota(jnp.int32, (LANES, LANES), 1)
+    g = jnp.dot(g_v[...], pick.astype(jnp.float32), precision=lax.Precision.HIGHEST, preferred_element_type=jnp.float32)
+    g_out[...] = g[0:own, 0:lx]
     for c in outs:
         c.wait()
 
@@ -481,7 +540,6 @@
         own = ly // mesh_sizes[2]
         tile = max(ROWS, own)
         any_spec = pl.BlockSpec(memory_space=pl.ANY)
-        smem = pl.BlockSpec(memory_space=pltpu.SMEM)
         vmem = pl.BlockSpec(memory_space=pltpu.VMEM)
         e, h, g = pl.pallas_call(
             lambda *refs: kernel(mesh_sizes, extent, *refs),
@@ -490,14 +548,12 @@
                 pltpu.VMEM((3, lx, ly, lz), f32),
                 pltpu.VMEM((tile, LANES), f32),
             ),
-            in_specs=[smem, smem, smem, vmem, any_spec, any_spec, any_spec, any_spec],
+            in_specs=[any_spec, any_spec, any_spec, any_spec, any_spec, any_spec, any_spec, any_spec],
             out_specs=(vmem, vmem, vmem),
             scratch_shapes=[
                 pltpu.VMEM(snapshots.shape, snapshots.dtype),
                 pltpu.VMEM((lx, ly, lz), jnp.int32),
                 pltpu.VMEM((lx, ly, lz), f32),
-                pltpu.VMEM((lx, ly, LANES), f32),
-                pltpu.VMEM((3, lx, ly, lz), f32),
                 pltpu.VMEM((STEPS, nport + 1, ly, lz), f32),
                 pltpu.VMEM((STEPS, 3, ly, lz), f32),
                 pltpu.VMEM((STEPS, 2, nt, lx, LANES), f32),
@@ -505,7 +561,8 @@
                 pltpu.VMEM((STEPS, 2, ly, lz), f32),
                 pltpu.VMEM((STEPS, 2, nt, lx, LANES), f32),
                 pltpu.VMEM((STEPS, ly, LANES), f32),
-                pltpu.VMEM((STEPS, 5, nt, lx, LANES), f32),
+                pltpu.VMEM((5, nt, lx, LANES), f32),
+                pltpu.VMEM((9, nt, lx, LANES), f32),
                 pltpu.VMEM((5, nt, lx, LANES), f32),
                 pltpu.VMEM((ly, LANES), f32),
                 pltpu.VMEM((STEPS, 2, ly, lz), f32),
@@ -521,7 +578,11 @@
                 pltpu.VMEM((STEPS, ROWS, LANES), f32),
                 pltpu.VMEM((STEPS, ly, LANES), f32),
                 pltpu.VMEM((3, tile, LANES), f32),
-                pltpu.SemaphoreType.DMA((2 + 2 * CHUNKS,)),
+                pltpu.SMEM(permittivity.shape, f32),
+                pltpu.SMEM(ports.shape, jnp.int32),
+                pltpu.SMEM(amplitudes.shape, f32),
+                pltpu.VMEM((ly, lx), jnp.int32),
+                pltpu.SemaphoreType.DMA((10,)),
                 pltpu.SemaphoreType.DMA((STEPS, 12)),
                 pltpu.SemaphoreType.DMA((STEPS, 12)),
                 pltpu.SemaphoreType.DMA((3,)),

time: 26.3 us -> 24.1 us (0.916)
  the two profiles are of different devices: /device:TPU:33 before, /device:TPU:97 now
where the time goes in v5:
time: 24.1 us; the launch traced here: 24 us
  Pallas kernels  23.4 us (97%)
  between operations  0.64 us (3%)
    pallas_call x1, Pallas kernels, body(): pl.pallas_call(lambda *refs: kernel(mesh_sizes, extent, *refs), out_shape...  21.1 us
    pallas_call x1, Pallas kernels, body(): pl.pallas_call(write_out, out_shape=(jax.ShapeDtypeStruct(e_adjoint.shape...  2.26 us

profile of v5, /device:TPU:97, one launch (start us, length us, event | category | flops | bytes accessed | tf_op | source)
XLA Modules:
  0.0 24.0 jit_solution(12665975978990488647)
XLA Ops:
  0.6 21.1 %reverse_steps.1 = (f32[3,33,16,256]{3,2,1,0:T(8,128)S(1)}, f32[3,32,16,256]{3,2,1,0:T(8,128)S(1)}, f32[8,128]{1,0:T(8,128)S(1)}) custom-call(f32[8]{0:T(128)} %refs_0_.1, s32[3]{0:T(128)} %refs_1_.1, f32[2,3]{1,0:T(2,128)} %refs_2_.1, s32[16,32]{1,0:T(8,128)} %bitcast.2, f32[3,32,16,256]{3,2,1,0:T(8,128)} %refs_4_.1, f32[3,32,16,256]{3,2,1,0:T(8,128)} %refs_5_.1, ...), custom_call_target="tpu_custom_call" | custom-call | tf_op jit(solution)/shard_map/reverse_steps/pallas_call | solution.py:544
  21.8 2.3 %write_out.1 = (f32[3,32,16,256]{3,2,1,0:T(8,128)}, f32[3,32,16,256]{3,2,1,0:T(8,128)}, f32[4,32]{1,0:T(4,128)}) custom-call(f32[3,33,16,256]{3,2,1,0:T(8,128)S(1)} %get-tuple-element.9.e_v, f32[3,32,16,256]{3,2,1,0:T(8,128)S(1)} %get-tuple-element.10.h_v, f32[8,128]{1,0:T(8,128)S(1)} %get-tuple-element.11.g_v), custom_call_target="tpu_custom_call" | custom-call | tf_op jit(solution)/shard_map/write_out/pallas_call | solution.py:595

commit v6 on v5

--- a/solution.py
+++ b/solution.py
@@ -10,7 +10,7 @@
 LANES = 128
 ROWS = 8
 half = 0.5
-U_MAG, U_PRE, U_POST, U_PACK = 8, 8, 8, 8
+U_MAG, U_PRE, U_POST, U_PACK = 8, 4, 8, 8
 
 EX, EY, EZ, PX, PY, PZ, D1, D2, D3, D4, D5, D6 = range(12)
 OFFSETS = (
@@ -60,7 +60,7 @@
         pltpu.make_async_copy(a, b, in_sem.at[6 + i])
         for i, (a, b) in enumerate(((perm_in, perm), (ports_in, ports), (amps_in, amps), (mask_in, mask_v)))
     ]
-    for c in [load_e[0], load_h[0], load_e[1], load_h[1]] + load_small + [load_m, load_s]:
+    for c in [load_e[0], load_h[0], load_e[1], load_h[1]] + load_small:
         c.start()
 
     barrier = pltpu.get_barrier_semaphore()
@@ -429,6 +429,8 @@
     top_y(0, *(wide(y_t[i]) for i in range(5)))
     send(PY, 0)
     load_e[1].wait()
+    load_m.start()
+    load_s.start()
     z_e[0] = lax.fori_loop(0, lx, first_pack, zero1, unroll=U_PACK)
     for msg in (EY, D4, D5, EZ):
         send(msg, 0)

time: 24.1 us -> 23.7 us (0.983)
  the two profiles are of different devices: /device:TPU:97 before, /device:TPU:160 now
where the time goes in v6:
time: 23.7 us; the launch traced here: 23.3 us
  Pallas kernels  22.7 us (96%)
  between operations  0.64 us (3%)
    pallas_call x1, Pallas kernels, body(): pl.pallas_call(lambda *refs: kernel(mesh_sizes, extent, *refs), out_shape...  20.4 us
    pallas_call x1, Pallas kernels, body(): pl.pallas_call(write_out, out_shape=(jax.ShapeDtypeStruct(e_adjoint.shape...  2.26 us

profile of v6, /device:TPU:160, one launch (start us, length us, event | category | flops | bytes accessed | tf_op | source)
XLA Modules:
  0.0 23.3 jit_solution(15354495006969450513)
XLA Ops:
  0.6 20.4 %reverse_steps.1 = (f32[3,33,16,256]{3,2,1,0:T(8,128)S(1)}, f32[3,32,16,256]{3,2,1,0:T(8,128)S(1)}, f32[8,128]{1,0:T(8,128)S(1)}) custom-call(f32[8]{0:T(128)} %refs_0_.1, s32[3]{0:T(128)} %refs_1_.1, f32[2,3]{1,0:T(2,128)} %refs_2_.1, s32[16,32]{1,0:T(8,128)} %bitcast.2, f32[3,32,16,256]{3,2,1,0:T(8,128)} %refs_4_.1, f32[3,32,16,256]{3,2,1,0:T(8,128)} %refs_5_.1, ...), custom_call_target="tpu_custom_call" | custom-call | tf_op jit(solution)/shard_map/reverse_steps/pallas_call | solution.py:546
  21.1 2.3 %write_out.1 = (f32[3,32,16,256]{3,2,1,0:T(8,128)}, f32[3,32,16,256]{3,2,1,0:T(8,128)}, f32[4,32]{1,0:T(4,128)}) custom-call(f32[3,33,16,256]{3,2,1,0:T(8,128)S(1)} %get-tuple-element.9.e_v, f32[3,32,16,256]{3,2,1,0:T(8,128)S(1)} %get-tuple-element.10.h_v, f32[8,128]{1,0:T(8,128)S(1)} %get-tuple-element.11.g_v), custom_call_target="tpu_custom_call" | custom-call | tf_op jit(solution)/shard_map/write_out/pallas_call | solution.py:597

commit v7 on v6

--- a/solution.py
+++ b/solution.py
@@ -10,7 +10,7 @@
 LANES = 128
 ROWS = 8
 half = 0.5
-U_MAG, U_PRE, U_POST, U_PACK = 8, 4, 8, 8
+U_MAG, U_PRE, U_POST, U_PACK, U_INNER = 8, 4, 8, 8, 6
 
 EX, EY, EZ, PX, PY, PZ, D1, D2, D3, D4, D5, D6 = range(12)
 OFFSETS = (
@@ -20,10 +20,14 @@
 )
 
 
+def rem(a, b):
+    return a % b if isinstance(a, int) else lax.rem(a, b)
+
+
 def kernel(mesh_sizes, extent, perm_in, ports_in, amps_in, mask_in, e_in, h_in, s_in, m_in,
            e_v, h_v, g_out,
            s_v, m_v, c_v, src_v,
-           x_e, y_e, z_e, x_p, y_p, z_p, y_t, y_b, rows_v, g_v,
+           x_e, y_e, z_e, x_p, y_p, z_p, y_t, y_b, d_r, d_s, rows_v, g_v,
            r_ex, r_ey, r_ez, r_px, r_py, r_pz, r_d1, r_d2, r_d3, r_d4, r_d5, r_d6, r_g,
            perm, ports, amps, mask_v, in_sem, send_sem, recv_sem, gs_sem, gr_sem):
     _, lx, ly, lz = e_in.shape
@@ -95,13 +99,13 @@
         if msg == D1:
             return e_in.at[0, lx - 1, :, 0:LANES] if first else x_e.at[phase, 2, :, 0:LANES]
         if msg == D2:
-            return e_in.at[0, lx - 1, 0:ROWS, :] if first else x_e.at[phase, 2, 0:ROWS, :]
+            return e_in.at[0, lx - 1, 0:ROWS, :] if first else d_r.at[0]
         if msg == D3:
-            return e_in.at[1, 0, ly - ROWS:ly, :] if first else x_e.at[phase, 0, ly - ROWS:ly, :]
+            return e_in.at[1, 0, ly - ROWS:ly, :] if first else d_r.at[1]
         if msg == D4:
-            return z_e.at[phase, ly - ROWS:ly, :]
+            return d_s.at[phase, 0]
         if msg == D5:
-            return z_e.at[phase, 0:ROWS, :]
+            return d_s.at[phase, 1]
         return e_in.at[2, 0, :, lz - LANES:lz] if first else x_e.at[phase, 1, :, lz - LANES:lz]
 
     def copy(msg, phase):
@@ -156,7 +160,7 @@
         return jnp.where(i == 0, 0.0, pltpu.roll(v, 1, axis))
 
     def pick(tile, from_lane, to, acc):
-        shift = lax.rem(to + (LANES - from_lane), LANES)
+        shift = rem(to + (LANES - from_lane), LANES)
         return jnp.where(lane1 == to, pltpu.roll(tile, shift, 1), acc)
 
     def put(dst, i, x, v, r):
@@ -167,19 +171,25 @@
         for k in range(nt):
             dst[i, k] = v[:, k * LANES:(k + 1) * LANES]
 
-    def pick_e(x, ex, ey, ez, acc):
+    def pick_e(x, ex, ey, acc):
         acc = pick(ex[:, 0:LANES], 0, 2 * x, acc)
-        acc = pick(ey[:, 0:LANES], 0, off + 2 * x, acc)
-        return pick(ez[:, lz - LANES:lz], LANES - 1, 2 * x + 1, acc)
+        return pick(ey[:, 0:LANES], 0, off + 2 * x, acc)
+
+    rx1 = lax.broadcasted_iota(jnp.int32, (lx, LANES), 0)
+    cx1 = lax.broadcasted_iota(jnp.int32, (lx, LANES), 1)
+
+    def lines(phase, ey, ez):
+        for i, (t, at_lane) in enumerate(((ey[:, 0:1], off), (ez[:, lz - 1:lz], 1))):
+            t = jnp.sum(jnp.where(cx1 == 2 * rx1 + at_lane, t, 0.0), axis=0, keepdims=True)
+            d_s[phase, i] = jnp.broadcast_to(t, (ROWS, LANES))
 
     def top_y(phase, ex, ey, ez, hx, hz):
         put_wide(y_p.at[phase], 0, hx + half * (ez + (up(ey, 1) - ey)))
         put_wide(y_p.at[phase], 1, hz - half * ((up(ey, 0) - ey) + ex))
 
-    def top_x(phase):
-        ex, ey, ez = e_v[0, lx - 1], e_v[1, lx - 1], e_v[2, lx - 1]
-        x_p[phase, 0] = h_v[1, lx - 1] - half * ((up(ex, 1) - ex) + ez)
-        x_p[phase, 1] = h_v[2, lx - 1] + half * (ey + (up(ex, 0) - ex))
+    def top_x(phase, ex, ey, ez, hy, hz):
+        x_p[phase, 0] = hy - half * ((up(ex, 1) - ex) + ez)
+        x_p[phase, 1] = hz + half * (ey + (up(ex, 0) - ex))
 
     def magnetic(phase):
         def one(x, acc):
@@ -258,6 +268,8 @@
 
     def halos(phase):
         fx, fy, fz = flags
+        for msg in (EX, PX, D1, D2):
+            wait_recv(msg, phase)
         d1 = pad_high(pltpu.roll(r_d1[phase], LANES - 1, 1))
         hy_x = (r_px[phase, 0] + half * x_e[phase, 1]) * fx - jnp.where(lane == lz - 1, half * d1, 0.0)
         d2 = jnp.broadcast_to(r_d2[phase, 0:1, :], (ly, lz))
@@ -274,6 +286,24 @@
         )
         for comp, x, d in planes:
             e_v[comp, x] = e_v[comp, x] + d
+        for msg in (EZ, PZ, D5, D6):
+            wait_recv(msg, phase)
+        own = pltpu.roll(z_e[phase], 1, 1)
+        low = lane1 < off
+        zh = (r_pz[phase] + jnp.where(low, -half * own, half * own)) * fz
+        d5 = jnp.broadcast_to(pltpu.roll(r_d5[phase], off, 1)[0:1, :], (ly, LANES))
+        zh = zh - jnp.where((row1 == ly - 1) & (lane1 >= off), half * d5, 0.0)
+        d6 = pltpu.roll(r_d6[phase], off, 1)
+        zh = zh + jnp.where(lane1 == off - 1, half * d6, 0.0)
+        ze = half * r_ez[phase]
+        odd = lax.rem(lane1, 2) == 1
+        cols = jnp.where(odd, jnp.where(low, zh, -zh), ze)
+        dhy = jnp.where(odd | (lane1 >= off), 0.0, -ze)
+        dhx = jnp.where(odd | (lane1 >= off), 0.0, pltpu.roll(ze, LANES - off, 1))
+        shift_x = jnp.where(lane1 < 2, 0.0, pltpu.roll(dhy, 2, 1))
+        last = (dhy - shift_x) - (dhx - down(dhx, 0))
+        for msg in (EY, PY, D3, D4):
+            wait_recv(msg, phase)
         rx = lax.broadcasted_iota(jnp.int32, (lx, LANES), 0)
         cx = lax.broadcasted_iota(jnp.int32, (lx, LANES), 1)
         d4 = jnp.broadcast_to(r_d4[phase, ROWS - 1:ROWS, :], (lx, LANES))
@@ -288,24 +318,8 @@
         values = (-hz_y, hx_y, dhz, (dhx - down(dhx, 1)) - (dhz - down(dhz, 0)), -dhx)
         for i, v in enumerate(values):
             put_wide(rows_v, i, v)
-        own = pltpu.roll(z_e[phase], 1, 1)
-        low = lane1 < off
-        zh = (r_pz[phase] + jnp.where(low, -half * own, half * own)) * fz
-        d5 = jnp.broadcast_to(pltpu.roll(r_d5[phase], off, 1)[0:1, :], (ly, LANES))
-        zh = zh - jnp.where((row1 == ly - 1) & (lane1 >= off), half * d5, 0.0)
-        d6 = pltpu.roll(r_d6[phase], off, 1)
-        zh = zh + jnp.where(lane1 == off - 1, half * d6, 0.0)
-        ze = half * r_ez[phase]
-        odd = lax.rem(lane1, 2) == 1
-        cols = jnp.where(odd, jnp.where(low, zh, -zh), ze)
-        dhy = jnp.where(odd | (lane1 >= off), 0.0, -ze)
-        dhx = jnp.where(odd | (lane1 >= off), 0.0, pltpu.roll(ze, LANES - off, 1))
-        shift_x = jnp.where(lane1 < 2, 0.0, pltpu.roll(dhy, 2, 1))
-        last = (dhy - shift_x) - (dhx - down(dhx, 0))
         return planes, values, cols, last
 
-    rx1 = lax.broadcasted_iota(jnp.int32, (lx, LANES), 0)
-    cx1 = lax.broadcasted_iota(jnp.int32, (lx, LANES), 1)
     cyw = lax.broadcasted_iota(jnp.int32, (lx, lz), 1)
 
     def first_rows(values, cols, last):
@@ -321,12 +335,17 @@
         b = [wide(y_b[i]) for i in range(9)]
         y, end = ly - 1, lz - 1
         hx_edge = edge(cols, y, off, end)
-        put_wide(y_e.at[1], 0, b[0] + b[7] * (values[0] + edge(cols, 0, 1, 0) + edge(cols, 0, 0, end)))
-        put_wide(y_e.at[1], 1, b[1] + b[7] * (values[1] + edge(last, 0, 0, end)))
+        ex0 = b[0] + b[7] * (values[0] + edge(cols, 0, 1, 0) + edge(cols, 0, 0, end))
+        ez0 = b[1] + b[7] * (values[1] + edge(last, 0, 0, end))
+        put_wide(y_e.at[1], 0, ex0)
+        put_wide(y_e.at[1], 1, ez0)
         ex = b[2] + b[8] * (values[2] + edge(cols, y, 1, 0) + edge(cols, y, 0, end))
         ey = b[3] + b[8] * (values[3] + edge(cols, y, off + 1, 0) + hx_edge)
         ez = b[4] + b[8] * (values[4] + edge(last, y, 0, end))
         top_y(1, ex, ey, ez, b[5] - values[4] + hx_edge, b[6] + values[2])
+        d_r[0] = jnp.broadcast_to(ex0[lx - 1:lx], (ROWS, lz))
+        d_r[1] = jnp.broadcast_to(ey[0:1], (ROWS, lz))
+        lines(1, ey, ez0)
 
     def gradient_part(planes, values, cols, last, acc_c, acc_l, acc_g):
         w = [wide(y_b[i]) for i in range(5)]
@@ -355,9 +374,9 @@
 
     def post(step, cols, last):
         def one(x, acc):
-            low_col = pltpu.roll(cols, lax.rem(2 * LANES - (2 * x + 1), LANES), 1)
-            high_col = pltpu.roll(cols, lax.rem(2 * LANES - (off + 2 * x + 1), LANES), 1)
-            last_col = pltpu.roll(last, lax.rem(2 * LANES - (2 * x + 1), LANES), 1)
+            low_col = pltpu.roll(cols, rem(2 * LANES - (2 * x + 1), LANES), 1)
+            high_col = pltpu.roll(cols, rem(2 * LANES - (off + 2 * x + 1), LANES), 1)
+            last_col = pltpu.roll(last, rem(2 * LANES - (2 * x + 1), LANES), 1)
             def delta(r, k, col0, col1, row0, row1_):
                 terms = []
                 cut = slice(r * ROWS, (r + 1) * ROWS)
@@ -404,9 +423,17 @@
                                 v = v + d if sign > 0 else v - d
                         if v is not None:
                             h_v[at_] = v
-            return pick_e(x, *(wide(n) for n in new), acc) if step + 1 < STEPS else acc
-
-        return lax.fori_loop(0, lx, one, zero1, unroll=U_POST)
+            return pick_e(x, wide(new[0]), wide(new[1]), acc) if step + 1 < STEPS else acc
+
+        if step + 1 == STEPS:
+            return lax.fori_loop(0, lx, one, zero1, unroll=U_POST)
+        acc = lax.fori_loop(0, lx, one, zero1, unroll=U_POST)
+        save_e(step + 1)
+        for msg in (D1, D6, EX):
+            send(msg, step + 1)
+        top_x(step + 1, e_v[0, lx - 1], e_v[1, lx - 1], e_v[2, lx - 1], h_v[1, lx - 1], h_v[2, lx - 1])
+        send(PX, step + 1)
+        return acc
 
     pl.semaphore_wait(barrier, count)
     for msg in (D2, D3, D1, D6, EX):
@@ -418,24 +445,26 @@
         return carry
 
     def first_pack(x, acc):
-        ex, ey, ez = e_v[0, x], e_v[1, x], e_v[2, x]
+        ex, ey = e_v[0, x], e_v[1, x]
         put(y_e.at[0], 0, x, ex, 0)
-        put(y_e.at[0], 1, x, ez, 0)
-        return pick_e(x, ex, ey, ez, acc)
+        put(y_e.at[0], 1, x, e_v[2, x], 0)
+        return pick_e(x, ex, ey, acc)
 
     load_e[0].wait()
     load_h[0].wait()
     lax.fori_loop(0, lx, first_top, 0, unroll=U_PACK)
-    top_y(0, *(wide(y_t[i]) for i in range(5)))
+    top_rows = [wide(y_t[i]) for i in range(5)]
+    top_y(0, *top_rows)
     send(PY, 0)
     load_e[1].wait()
     load_m.start()
     load_s.start()
     z_e[0] = lax.fori_loop(0, lx, first_pack, zero1, unroll=U_PACK)
+    lines(0, top_rows[1], wide(y_e[0, 1]))
     for msg in (EY, D4, D5, EZ):
         send(msg, 0)
     load_h[1].wait()
-    top_x(0)
+    top_x(0, e_v[0, lx - 1], e_v[1, lx - 1], e_v[2, lx - 1], h_v[1, lx - 1], h_v[2, lx - 1])
     send(PX, 0)
     magnetic(0)
     send(PZ, 0)
@@ -460,27 +489,18 @@
     coefs = [half / jnp.full((ly, lz), perm[k], f32) for k in range(nmat)]
     load_m.wait()
     pre(0)
-    for msg in range(12):
-        wait_recv(msg, 0)
     planes, values, cols, last = halos(0)
     first_rows(values, cols, last)
-    for msg in (EY, PY):
+    for msg in (EY, PY, D2, D3, D4, D5):
         send(msg, 1)
     z_e[1] = post(0, cols, last)
-    save_e(1)
-    for msg in (D2, D3, D1, D6, D4, D5, EX):
-        send(msg, 1)
-    top_x(1)
-    for msg in (PX, EZ):
-        send(msg, 1)
+    send(EZ, 1)
     magnetic(1)
     send(PZ, 1)
     load_s.wait()
     weights = pre(1)
     spread = lax.broadcasted_iota(jnp.int32, (lx, LANES), 1) == 2 * lax.broadcasted_iota(jnp.int32, (lx, LANES), 0)
     mask = jnp.dot(mask_v[...].astype(f32), spread.astype(f32), preferred_element_type=f32)
-    for msg in range(12):
-        wait_recv(msg, 1)
     planes, values, cols, last = halos(1)
     acc = gradient_part(planes, values, cols, last, *weights)
 
@@ -565,6 +585,8 @@
                 pltpu.VMEM((STEPS, ly, LANES), f32),
                 pltpu.VMEM((5, nt, lx, LANES), f32),
                 pltpu.VMEM((9, nt, lx, LANES), f32),
+                pltpu.VMEM((2, ROWS, lz), f32),
+                pltpu.VMEM((STEPS, 2, ROWS, LANES), f32),
                 pltpu.VMEM((5, nt, lx, LANES), f32),
                 pltpu.VMEM((ly, LANES), f32),
                 pltpu.VMEM((STEPS, 2, ly, lz), f32),

time: 23.7 us -> 23.8 us (level)
  no operation moved by 1% of the time
where the time goes in v7:
time: 23.8 us; the launch traced here: 23.3 us
  Pallas kernels  22.7 us (95%)
  between operations  0.64 us (3%)
    pallas_call x1, Pallas kernels, body(): pl.pallas_call(lambda *refs: kernel(mesh_sizes, extent, *refs), out_shape...  20.4 us
    pallas_call x1, Pallas kernels, body(): pl.pallas_call(write_out, out_shape=(jax.ShapeDtypeStruct(e_adjoint.shape...  2.26 us

profile of v7, /device:TPU:160, one launch (start us, length us, event | category | flops | bytes accessed | tf_op | source)
XLA Modules:
  0.0 23.3 jit_solution(6982655493960711197)
XLA Ops:
  0.6 20.4 %reverse_steps.1 = (f32[3,33,16,256]{3,2,1,0:T(8,128)S(1)}, f32[3,32,16,256]{3,2,1,0:T(8,128)S(1)}, f32[8,128]{1,0:T(8,128)S(1)}) custom-call(f32[8]{0:T(128)} %refs_0_.1, s32[3]{0:T(128)} %refs_1_.1, f32[2,3]{1,0:T(2,128)} %refs_2_.1, s32[16,32]{1,0:T(8,128)} %bitcast.2, f32[3,32,16,256]{3,2,1,0:T(8,128)} %refs_4_.1, f32[3,32,16,256]{3,2,1,0:T(8,128)} %refs_5_.1, ...), custom_call_target="tpu_custom_call" | custom-call | tf_op jit(solution)/shard_map/reverse_steps/pallas_call | solution.py:566
  21.0 2.3 %write_out.1 = (f32[3,32,16,256]{3,2,1,0:T(8,128)}, f32[3,32,16,256]{3,2,1,0:T(8,128)}, f32[4,32]{1,0:T(4,128)}) custom-call(f32[3,33,16,256]{3,2,1,0:T(8,128)S(1)} %get-tuple-element.9.e_v, f32[3,32,16,256]{3,2,1,0:T(8,128)S(1)} %get-tuple-element.10.h_v, f32[8,128]{1,0:T(8,128)S(1)} %get-tuple-element.11.g_v), custom_call_target="tpu_custom_call" | custom-call | tf_op jit(solution)/shard_map/write_out/pallas_call | solution.py:619
